TPU v7x, 128 devices: a whole 4x4x4 slice. The times are simulated.
128 devices in a mesh: gx: 4 (over z), gy: 32 (over y, x, core).
Axes of the slice: x: 4, y: 4, z: 4, core: 2. Of those that a mesh axis runs over, the one named last changes fastest.
Arguments:
- blocks: float32 [768, 128, 4096], P(('gx', 'gy')), may hold values from -0.046875 to 0.046875
- features: float32 [2048, 128, 512], P(('gx', 'gy')), may hold values from -6 to 6
- col_ids: int32 [768, 32], P(('gx', 'gy')), may hold values from 0 to 15
- row_ids: int32 [768], P(('gx', 'gy')), may hold values from 0 to 127
- factor: float32 [512, 512], replicated, may hold values from -0.25 to 0.25
Outputs:
- owned_rows: float32 [16384, 512], P(('gx', 'gy'))
- returned: float32 [98304, 512], P(('gx', 'gy'))
Inputs may be any that keep to these rules, and one draw needn't show every extreme that they name: `row_ids`: row block r is owned by device r, counted over gx+gy with gx slowest. Row blocks are named with a power-law skew; one device may name a row block more than once. `col_ids`: indices into the device's own feature tiles.
All inputs are finite; a program needn't handle non-finite values.
Results may differ from a plain program's by a relative error of at most 0.00013.
Values sent between devices are 32-bit elements; how exact they have to be, the bound alone decides.
A program may use at most 192 MiB of HBM per device.

v0:
```python
import jax
import jax.numpy as jnp
from jax import lax
from jax.sharding import PartitionSpec as P

HIGHEST = lax.Precision.HIGHEST


def partner(value, axis, bit):
    mask = 2**bit
    pairs = [(source, source ^ mask) for source in range(lax.axis_size(axis))]
    return lax.ppermute(value, axis, pairs)


def to_dense(labels, values, range_base, range_size):
    one_hot = (
        labels[None, :] - range_base == jnp.arange(range_size, dtype=jnp.int32)[:, None]
    ).astype(jnp.float32)
    flat = values.reshape(values.shape[0], -1)
    summed = jnp.einsum("sk,kx->sx", one_hot, flat, precision=HIGHEST)
    return summed.reshape((range_size,) + values.shape[1:])


def from_dense(labels, dense_rows, range_base):
    range_size = dense_rows.shape[0]
    one_hot = (
        labels[:, None] - range_base == jnp.arange(range_size, dtype=jnp.int32)[None, :]
    ).astype(jnp.float32)
    flat = dense_rows.reshape(range_size, -1)
    picked = jnp.einsum("ks,sx->kx", one_hot, flat, precision=HIGHEST)
    return picked.reshape((labels.shape[0],) + dense_rows.shape[1:])


def local(blocks, features, col_ids, row_ids, factor):
    slot_count = row_ids.shape[0]
    tile_rows = blocks.shape[1]
    feat_width = features.shape[2]
    per_row = col_ids.shape[1]
    levels = (lax.axis_size("gx") * lax.axis_size("gy")).bit_length() - 1
    my_index = lax.axis_index("gx") * lax.axis_size("gy") + lax.axis_index("gy")
    partial_rows = []
    for slot_num in range(slot_count):
        stacked = features[col_ids[slot_num]].reshape(per_row * tile_rows, feat_width)
        partial_rows.append(
            jnp.dot(
                blocks[slot_num], stacked, precision=HIGHEST, preferred_element_type=jnp.float32
            )
        )
    values = jnp.stack(partial_rows)
    labels = row_ids
    dense_rows = None
    records = []
    for section_num in range(levels):
        bit_level = levels - 1 - section_num
        my_bit = my_index >> bit_level & 1
        if dense_rows is None:
            valid = labels >= 0
            kept_mask = (labels >> bit_level & 1 == my_bit) & valid
            sent_mask = jnp.logical_not(kept_mask) & valid
            send_labels = jnp.where(sent_mask, labels, -1).astype(jnp.float32)
            send_values = jnp.where(sent_mask[:, None, None], values, 0.0)
            got_labels, got_values = partner((send_labels, send_values), ("gx", "gy"), bit_level)
            labels = jnp.concatenate(
                [jnp.where(kept_mask, labels, -1), got_labels.astype(jnp.int32)]
            )
            values = jnp.concatenate([jnp.where(kept_mask[:, None, None], values, 0.0), got_values])
            records.append(("list", kept_mask, 0, bit_level))
            if labels.shape[0] > 2**bit_level:
                range_base = my_index >> bit_level << bit_level
                dense_rows = to_dense(labels, values, range_base, 2**bit_level)
                records.append(("lookup", labels, range_base, 0))
        else:
            half_size = dense_rows.shape[0] // 2
            is_upper = my_bit == 1
            outgoing = jnp.where(is_upper, dense_rows[:half_size], dense_rows[half_size:])
            staying = jnp.where(is_upper, dense_rows[half_size:], dense_rows[:half_size])
            dense_rows = staying + partner(outgoing, ("gx", "gy"), bit_level)
            records.append(("halve", is_upper, 0, bit_level))
    owned_rows = jnp.dot(
        jnp.tanh(dense_rows[0]), factor, precision=HIGHEST, preferred_element_type=jnp.float32
    )
    answers = owned_rows[None]
    for record in reversed(records):
        if record[0] == "halve":
            is_upper = record[1]
            incoming = partner(answers, ("gx", "gy"), record[3])
            answers = jnp.where(
                is_upper, jnp.concatenate([incoming, answers]), jnp.concatenate([answers, incoming])
            )
        elif record[0] == "lookup":
            answers = from_dense(record[1], answers, record[2])
        else:
            kept_mask = record[1]
            count_kept = kept_mask.shape[0]
            incoming = partner(answers[count_kept:], ("gx", "gy"), record[3])
            answers = jnp.where(kept_mask[:, None, None], answers[:count_kept], incoming)
    returned = answers.reshape(slot_count * tile_rows, feat_width)
    return (owned_rows, returned)


def solution(mesh):
    return jax.shard_map(
        local,
        mesh=mesh,
        in_specs=(
            P(("gx", "gy"), None, None),
            P(("gx", "gy"), None, None),
            P(("gx", "gy"), None),
            P(("gx", "gy")),
            P(),
        ),
        out_specs=(P(("gx", "gy"), None), P(("gx", "gy"), None)),
        check_vma=False,
    )
```

profile of v0, /device:TPU:1, one launch (start us, length us, event | category | flops | bytes accessed | tf_op | source)
XLA Modules:
  0.0 887.0 jit_solution(2355823613509592494)
XLA Ops:
  0.6 0.9 fusion.78
  1.6 6.6 gather_fusion
  8.1 6.5 gather_fusion.1
  14.7 6.6 gather_fusion.2
  21.2 6.5 gather_fusion.3
  27.7 6.5 gather_fusion.4
  34.3 6.5 gather_fusion.5
  40.8 16.0 %fusion.32 = f32[6,128,512]{1,2,0:T(8,128)S(1)} fusion(f32[4096,512]{1,0:T(8,128)} %bitcast.143, f32[6,128,4096]{2,1,0:T(8,128)} %param.5), kind=kOutput, calls=%fused_computation.47 | convolution fusion | flops 3221225472 | bytes 10747904 | tf_op jit(solution)/shard_map/dot_general | solution.py:45
  56.8 16.6 %fusion.38 = f32[6,128,512]{1,2,0:T(8,128)S(1)} fusion(f32[6,128,512]{1,2,0:T(8,128)S(1)} %fusion.32, f32[4096,512]{1,0:T(8,128)} %bitcast.144, f32[6,128,4096]{2,1,0:T(8,128)} %param.5), kind=kOutput, calls=%fused_computation.49 | convolution fusion | flops 3221225472 | bytes 10747904 | tf_op jit(solution)/shard_map/dot_general | solution.py:45
  73.5 15.0 %fusion.44 = f32[6,128,512]{1,2,0:T(8,128)S(1)} fusion(f32[6,128,512]{1,2,0:T(8,128)S(1)} %fusion.38, f32[4096,512]{1,0:T(8,128)S(1)} %bitcast.147, f32[6,128,4096]{2,1,0:T(8,128)} %param.5), kind=kOutput, calls=%fused_computation.51 | convolution fusion | flops 3221225472 | bytes 10747904 | tf_op jit(solution)/shard_map/dot_general | solution.py:45
  88.6 15.1 %fusion.50 = f32[6,128,512]{1,2,0:T(8,128)S(1)} fusion(f32[6,128,512]{1,2,0:T(8,128)S(1)} %fusion.44, f32[4096,512]{1,0:T(8,128)S(1)} %bitcast.150, f32[6,128,4096]{2,1,0:T(8,128)} %param.5), kind=kOutput, calls=%fused_computation.53 | convolution fusion | flops 3221225472 | bytes 10747904 | tf_op jit(solution)/shard_map/dot_general | solution.py:45
  103.7 15.3 %fusion.56 = f32[6,128,512]{1,2,0:T(8,128)S(1)} fusion(f32[6,128,512]{1,2,0:T(8,128)S(1)} %fusion.50, f32[4096,512]{1,0:T(8,128)S(1)} %bitcast.153, f32[6,128,4096]{2,1,0:T(8,128)} %param.5), kind=kOutput, calls=%fused_computation.55 | convolution fusion | flops 3221225472 | bytes 10747904 | tf_op jit(solution)/shard_map/dot_general | solution.py:45
  119.0 14.9 %fusion.62 = f32[6,128,512]{1,2,0:T(8,128)S(1)} fusion(f32[6,128,512]{1,2,0:T(8,128)S(1)} %fusion.56, f32[4096,512]{1,0:T(8,128)S(1)} %bitcast.156, f32[6,128,4096]{2,1,0:T(8,128)} %param.5), kind=kOutput, calls=%fused_computation.57 | convolution fusion | flops 3221225472 | bytes 10747904 | tf_op jit(solution)/shard_map/dot_general | solution.py:45
  133.9 1.5 broadcast_select_fusion.2
  135.4 4.4 collective-permute-start.3
  139.9 34.3 %collective-permute-done = f32[6]{0:T(128)S(1)} collective-permute-done((f32[6]{0:T(128)S(1)}, f32[6]{0:T(128)S(1)}, u32[]{:S(2)}, u32[]{:S(2)}) %collective-permute-start) | collective-permute-done | bytes 56 | tf_op jit(solution)/shard_map/ppermute | solution.py:12
  174.3 4.7 fusion.9
  179.8 0.7 collective-permute-start.1
  180.5 67.3 %collective-permute-done.1 = f32[12]{0:T(128)S(1)} collective-permute-done((f32[12]{0:T(128)S(1)}, f32[12]{0:T(128)S(1)}, u32[]{:S(2)}, u32[]{:S(2)}) %collective-permute-start.1) | collective-permute-done | bytes 80 | tf_op jit(solution)/shard_map/ppermute | solution.py:12
  247.9 9.1 %fusion.1 = (f32[24,128,512]{1,2,0:T(8,128)}, f32[24,128,512]{1,2,0:T(8,128)}) fusion(f32[12,128,512]{1,2,0:T(8,128)} %collective-permute-done.4, f32[12,128,512]{1,2,0:T(8,128)} %get-tuple-element.16, pred[24]{0:T(512)(128)(4,1)S(1)} %get-tuple-element.3, pred[24]{0:T(512)(128)(4,1)S(1)} %not_and_fusion), kind=kLoop, calls=%fused_computation.9 | loop fusion | flops 4718592 | bytes 18874416 | tf_op jit(solution)/shard_map/jit(_where)/select_n | solution.py:66
  257.0 2.9 collective-permute-start.5
  260.1 133.8 %collective-permute-done.2 = f32[24]{0:T(128)S(1)} collective-permute-done((f32[24]{0:T(128)S(1)}, f32[24]{0:T(128)S(1)}, u32[]{:S(2)}, u32[]{:S(2)}) %collective-permute-start.2) | collective-permute-done | bytes 128 | tf_op jit(solution)/shard_map/ppermute | solution.py:12
  393.9 10.6 %pad_maximum_fusion = f32[48,128,512]{1,2,0:T(8,128)} fusion(f32[24,128,512]{1,2,0:T(8,128)} %collective-permute-done.5, f32[24,128,512]{1,2,0:T(8,128)} %get-tuple-element.12), kind=kLoop, calls=%fused_computation.6 | loop fusion | flops 3145728 | bytes 25165824 | tf_op jit(solution)/shard_map/concatenate | solution.py:66
  404.5 12.7 %copy.12 = f32[6,8,128,512]{3,1,2,0:T(8,128)} copy(f32[6,8,128,512]{2,3,1,0:T(8,128)} %bitcast.141) | data formatting | bytes 25165824
  417.2 7.4 fusion.71
  424.6 2.3 slice_select_fusion.1
  426.9 1.3 collective-permute-start.6
  428.2 43.2 %collective-permute-done.6 = f32[8,128,512]{2,0,1:T(8,128)S(1)} collective-permute-done((f32[8,128,512]{2,0,1:T(8,128)}, f32[8,128,512]{2,0,1:T(8,128)S(1)}, u32[]{:S(2)}, u32[]{:S(2)}) %collective-permute-start.6) | collective-permute-done | bytes 2097184 | tf_op jit(solution)/shard_map/ppermute | solution.py:12
  471.4 1.3 copy-done.3
  472.7 2.7 add.82
  475.4 1.2 slice_select_fusion.4
  476.6 2.7 collective-permute-start.7
  479.4 20.0 %collective-permute-done.7 = f32[4,128,512]{2,0,1:T(4,128)} collective-permute-done((f32[4,128,512]{2,0,1:T(4,128)}, f32[4,128,512]{2,0,1:T(4,128)}, u32[]{:S(2)}, u32[]{:S(2)}) %collective-permute-start.7) | collective-permute-done | bytes 1048608 | tf_op jit(solution)/shard_map/ppermute | solution.py:12
  499.4 1.6 select_add_fusion
  501.0 1.0 copy-done.1
  502.2 1.3 collective-permute-start.8
  503.5 7.6 collective-permute-done.8
  511.1 2.1 select_add_fusion.1
  513.5 5.8 collective-permute-start.9
  519.3 1.2 collective-permute-done.9
  522.3 0.9 collective-permute-done.10
  523.2 1.3 collective-permute-start.11
  524.8 0.7 maximum_select_fusion.7
  525.5 10.9 %collective-permute-done.11 = f32[2,128,512]{2,1,0:T(8,128)S(1)} collective-permute-done((f32[2,128,512]{2,1,0:T(8,128)S(1)}, f32[2,128,512]{2,1,0:T(8,128)S(1)}, u32[]{:S(2)}, u32[]{:S(2)}) %collective-permute-start.11) | collective-permute-done | bytes 524320 | tf_op jit(solution)/shard_map/ppermute | solution.py:12
  536.5 2.8 collective-permute-start.12
  539.8 0.7 maximum_select_fusion.5
  540.5 21.1 %collective-permute-done.12 = f32[4,128,512]{2,1,0:T(8,128)S(1)} collective-permute-done((f32[4,128,512]{2,1,0:T(8,128)S(1)}, f32[4,128,512]{2,1,0:T(8,128)S(1)}, u32[]{:S(2)}, u32[]{:S(2)}) %collective-permute-start.12) | collective-permute-done | bytes 1048608 | tf_op jit(solution)/shard_map/ppermute | solution.py:12
  561.9 1.3 collective-permute-start.13
  563.9 0.7 maximum_select_fusion.3
  564.7 42.4 %collective-permute-done.13 = f32[8,128,512]{2,1,0:T(8,128)S(1)} collective-permute-done((f32[8,128,512]{2,1,0:T(8,128)S(1)}, f32[8,128,512]{2,1,0:T(8,128)S(1)}, u32[]{:S(2)}, u32[]{:S(2)}) %collective-permute-start.13) | collective-permute-done | bytes 2097184 | tf_op jit(solution)/shard_map/ppermute | solution.py:12
  607.1 1.2 copy.13
  608.3 8.0 fusion.2
  616.3 9.9 %fusion.80 = (f32[24,65536]{1,0:T(8,128)}, f32[24,65536]{1,0:T(8,128)}) fusion(f32[48,65536]{1,0:T(8,128)} %fusion.2), kind=kLoop, calls=%fused_computation.114 | loop fusion | bytes 25165824 | tf_op jit(solution)/shard_map/slice | solution.py:95
  626.2 9.1 %copy.19 = f32[3,8,128,512]{3,2,1,0:T(8,128)} copy(f32[3,8,128,512]{3,1,2,0:T(8,128)} %bitcast.160) | data formatting | bytes 12582912
  635.3 6.6 copy.8
  641.9 3.1 collective-permute-start.14
  645.0 9.1 %copy.18 = f32[3,8,128,512]{3,2,1,0:T(8,128)} copy(f32[3,8,128,512]{3,1,2,0:T(8,128)} %bitcast.159) | data formatting | bytes 12582912
  654.1 6.6 copy.9
  660.6 117.4 %collective-permute-done.14 = f32[24,128,512]{1,2,0:T(8,128)} collective-permute-done((f32[24,128,512]{1,2,0:T(8,128)}, f32[24,128,512]{1,2,0:T(8,128)}, u32[]{:S(2)}, u32[]{:S(2)}) %collective-permute-start.14) | collective-permute-done | bytes 6291488 | tf_op jit(solution)/shard_map/ppermute | solution.py:12
  778.1 5.4 broadcast_select_fusion
  783.8 65.8 %collective-permute-done.15 = f32[12,128,512]{1,2,0:T(8,128)S(1)} collective-permute-done((f32[12,128,512]{1,2,0:T(8,128)S(1)}, f32[12,128,512]{1,2,0:T(8,128)S(1)}, u32[]{:S(2)}, u32[]{:S(2)}) %collective-permute-start.15) | collective-permute-done | bytes 3145760 | tf_op jit(solution)/shard_map/ppermute | solution.py:12
  850.3 1.7 collective-permute-start.16
  852.0 32.6 %collective-permute-done.16 = f32[6,128,512]{1,2,0:T(8,128)S(1)} collective-permute-done((f32[6,128,512]{1,2,0:T(8,128)S(1)}, f32[6,128,512]{1,2,0:T(8,128)S(1)}, u32[]{:S(2)}, u32[]{:S(2)}) %collective-permute-start.16) | collective-permute-done | bytes 1572896 | tf_op jit(solution)/shard_map/ppermute | solution.py:12
  884.9 1.6 copy.10
  (67 shorter events, 6.7 us)
Async XLA Ops:
  0.6 520.2 %copy-start = (f32[512,512]{1,0:T(8,128)S(1)}, f32[512,512]{1,0:T(8,128)}, u32[]{:S(2)}) copy-start(f32[512,512]{1,0:T(8,128)} %param.9) | copy-start | bytes 3145732
  34.3 6.5 copy-start.4
  40.8 32.6 %slice-start = ((s8[8388608]{0:T(1024)(128)(4,1)}), s8[4194304]{0:T(1024)(128)(4,1)S(1)}, s32[]{:S(2)}) async-start(s8[8388608]{0:T(1024)(128)(4,1)} %bitcast.145), calls=%async_computation | async-start | bytes 8388608
  56.8 16.7 %slice-start.1 = ((s8[8388608]{0:T(1024)(128)(4,1)}), s8[4194304]{0:T(1024)(128)(4,1)S(1)}, s32[]{:S(2)}) async-start(s8[8388608]{0:T(1024)(128)(4,1)} %bitcast.145), calls=%async_computation.1 | async-start | bytes 8388608
  56.8 31.7 %slice-start.2 = ((s8[8388608]{0:T(1024)(128)(4,1)}), s8[4194304]{0:T(1024)(128)(4,1)S(1)}, s32[]{:S(2)}) async-start(s8[8388608]{0:T(1024)(128)(4,1)} %bitcast.148), calls=%async_computation.2 | async-start | bytes 8388608
  73.5 15.1 %slice-start.3 = ((s8[8388608]{0:T(1024)(128)(4,1)}), s8[4194304]{0:T(1024)(128)(4,1)S(1)}, s32[]{:S(2)}) async-start(s8[8388608]{0:T(1024)(128)(4,1)} %bitcast.148), calls=%async_computation.3 | async-start | bytes 8388608
  73.5 30.2 %slice-start.4 = ((s8[8388608]{0:T(1024)(128)(4,1)}), s8[4194304]{0:T(1024)(128)(4,1)S(1)}, s32[]{:S(2)}) async-start(s8[8388608]{0:T(1024)(128)(4,1)} %bitcast.151), calls=%async_computation.4 | async-start | bytes 8388608
  88.6 15.1 %slice-start.5 = ((s8[8388608]{0:T(1024)(128)(4,1)}), s8[4194304]{0:T(1024)(128)(4,1)S(1)}, s32[]{:S(2)}) async-start(s8[8388608]{0:T(1024)(128)(4,1)} %bitcast.151), calls=%async_computation.5 | async-start | bytes 8388608
  88.6 30.4 %slice-start.6 = ((s8[8388608]{0:T(1024)(128)(4,1)}), s8[4194304]{0:T(1024)(128)(4,1)S(1)}, s32[]{:S(2)}) async-start(s8[8388608]{0:T(1024)(128)(4,1)} %bitcast.154), calls=%async_computation.6 | async-start | bytes 8388608
  103.7 15.3 %slice-start.7 = ((s8[8388608]{0:T(1024)(128)(4,1)}), s8[4194304]{0:T(1024)(128)(4,1)S(1)}, s32[]{:S(2)}) async-start(s8[8388608]{0:T(1024)(128)(4,1)} %bitcast.154), calls=%async_computation.7 | async-start | bytes 8388608
  135.4 38.9 %collective-permute-start.3 = (f32[6,128,512]{1,2,0:T(8,128)}, f32[6,128,512]{1,2,0:T(8,128)}, u32[]{:S(2)}, u32[]{:S(2)}) collective-permute-start(f32[6,128,512]{1,2,0:T(8,128)} %get-tuple-element.19), channel_id=1, source_target_pairs={{0,64},{1,65},{2,66},{3,67},{4,68},{5,69},{6,70},{7,71},{8,72},{9,... | collective-permute-start | bytes 4718600 | tf_op jit(solution)/shard_map/ppermute | solution.py:12
  139.8 34.4 %collective-permute-start = (f32[6]{0:T(128)S(1)}, f32[6]{0:T(128)S(1)}, u32[]{:S(2)}, u32[]{:S(2)}) collective-permute-start(f32[6]{0:T(128)S(1)} %select_convert_fusion.2), channel_id=1, source_target_pairs={{0,64},{1,65},{2,66},{3,67},{4,68},{5,69},{6,70},{7,71},{8,72},{9,... | collective-permute-start | bytes 80 | tf_op jit(solution)/shard_map/ppermute | solution.py:12
  179.1 68.8 %collective-permute-start.4 = (f32[12,128,512]{1,2,0:T(8,128)}, f32[12,128,512]{1,2,0:T(8,128)}, u32[]{:S(2)}, u32[]{:S(2)}) collective-permute-start(f32[12,128,512]{1,2,0:T(8,128)} %get-tuple-element.17), channel_id=1, source_target_pairs={{0,32},{1,33},{2,34},{3,35},{4,36},{5,37},{6,38},{7,39},{8,40},{9,... | collective-permute-start | bytes 9437192 | tf_op jit(solution)/shard_map/ppermute | solution.py:12
  179.8 68.0 %collective-permute-start.1 = (f32[12]{0:T(128)S(1)}, f32[12]{0:T(128)S(1)}, u32[]{:S(2)}, u32[]{:S(2)}) collective-permute-start(f32[12]{0:T(128)S(1)} %select_convert_fusion.1), channel_id=1, source_target_pairs={{0,32},{1,33},{2,34},{3,35},{4,36},{5,37},{6,38},{7,39},{8,40},{9,... | collective-permute-start | bytes 152 | tf_op jit(solution)/shard_map/ppermute | solution.py:12
  257.0 136.9 %collective-permute-start.5 = (f32[24,128,512]{1,2,0:T(8,128)}, f32[24,128,512]{1,2,0:T(8,128)}, u32[]{:S(2)}, u32[]{:S(2)}) collective-permute-start(f32[24,128,512]{1,2,0:T(8,128)} %get-tuple-element.13), channel_id=1, source_target_pairs={{0,16},{1,17},{2,18},{3,19},{4,20},{5,21},{6,22},{7,23},{8,24},{9,... | collective-permute-start | bytes 18874376 | tf_op jit(solution)/shard_map/ppermute | solution.py:12
  260.0 133.9 %collective-permute-start.2 = (f32[24]{0:T(128)S(1)}, f32[24]{0:T(128)S(1)}, u32[]{:S(2)}, u32[]{:S(2)}) collective-permute-start(f32[24]{0:T(128)S(1)} %select_convert_fusion), channel_id=1, source_target_pairs={{0,16},{1,17},{2,18},{3,19},{4,20},{5,21},{6,22},{7,23},{8,24},{9,... | collective-permute-start | bytes 296 | tf_op jit(solution)/shard_map/ppermute | solution.py:12
  426.9 44.5 %collective-permute-start.6 = (f32[8,128,512]{2,0,1:T(8,128)}, f32[8,128,512]{2,0,1:T(8,128)S(1)}, u32[]{:S(2)}, u32[]{:S(2)}) collective-permute-start(f32[8,128,512]{2,0,1:T(8,128)} %bitcast.37), channel_id=1, source_target_pairs={{0,8},{1,9},{2,10},{3,11},{4,12},{5,13},{6,14},{7,15},{8,0},{9,1},... | collective-permute-start | bytes 6291464 | tf_op jit(solution)/shard_map/ppermute | solution.py:12
  471.4 1.3 copy-start.3
  476.6 22.7 %collective-permute-start.7 = (f32[4,128,512]{2,0,1:T(4,128)}, f32[4,128,512]{2,0,1:T(4,128)}, u32[]{:S(2)}, u32[]{:S(2)}) collective-permute-start(f32[4,128,512]{2,0,1:T(4,128)} %slice_select_fusion.4), channel_id=1, source_target_pairs={{0,4},{1,5},{2,6},{3,7},{4,0},{5,1},{6,2},{7,3},{8,12},{9,13},{10,... | collective-permute-start | bytes 3145736 | tf_op jit(solution)/shard_map/ppermute | solution.py:12
  500.9 1.0 copy-start.1
  502.2 8.9 %collective-permute-start.8 = (f32[2,128,512]{2,0,1:T(2,128)S(1)}, f32[2,128,512]{2,0,1:T(2,128)S(1)}, u32[]{:S(2)}, u32[]{:S(2)}) collective-permute-start(f32[2,128,512]{2,0,1:T(2,128)S(1)} %broadcast_select_fusion.3), channel_id=1, source_target_pairs={{0,2},{1,3},{2,0},{3,1},{4,6},{5,7},{6,4},{7,5},{8,10},{9,11},{10,... | collective-permute-start | bytes 1572872 | tf_op jit(solution)/shard_map/ppermute | solution.py:12
  513.5 7.0 collective-permute-start.9
  521.5 19.0 %copy-start.2 = (f32[128,512]{1,0:T(8,128)}, f32[128,512]{1,0:T(8,128)S(1)}, u32[]{:S(2)}) copy-start(f32[128,512]{1,0:T(8,128)S(1)} %fusion.67) | copy-start | bytes 786436
  521.5 1.6 collective-permute-start.10
  523.2 13.2 %collective-permute-start.11 = (f32[2,128,512]{2,1,0:T(8,128)S(1)}, f32[2,128,512]{2,1,0:T(8,128)S(1)}, u32[]{:S(2)}, u32[]{:S(2)}) collective-permute-start(f32[2,128,512]{2,1,0:T(8,128)S(1)} %maximum_select_fusion.6), channel_id=1, source_target_pairs={{0,2},{1,3},{2,0},{3,1},{4,6},{5,7},{6,4},{7,5},{8,10},{9,11},{10,... | collective-permute-start | bytes 1572872 | tf_op jit(solution)/shard_map/ppermute | solution.py:12
  536.5 25.1 %collective-permute-start.12 = (f32[4,128,512]{2,1,0:T(8,128)S(1)}, f32[4,128,512]{2,1,0:T(8,128)S(1)}, u32[]{:S(2)}, u32[]{:S(2)}) collective-permute-start(f32[4,128,512]{2,1,0:T(8,128)S(1)} %maximum_select_fusion.4), channel_id=1, source_target_pairs={{0,4},{1,5},{2,6},{3,7},{4,0},{5,1},{6,2},{7,3},{8,12},{9,13},{10,... | collective-permute-start | bytes 3145736 | tf_op jit(solution)/shard_map/ppermute | solution.py:12
  561.9 45.2 %collective-permute-start.13 = (f32[8,128,512]{2,1,0:T(8,128)S(1)}, f32[8,128,512]{2,1,0:T(8,128)S(1)}, u32[]{:S(2)}, u32[]{:S(2)}) collective-permute-start(f32[8,128,512]{2,1,0:T(8,128)S(1)} %maximum_select_fusion.2), channel_id=1, source_target_pairs={{0,8},{1,9},{2,10},{3,11},{4,12},{5,13},{6,14},{7,15},{8,0},{9,1},... | collective-permute-start | bytes 6291464 | tf_op jit(solution)/shard_map/ppermute | solution.py:12
  641.9 136.2 %collective-permute-start.14 = (f32[24,128,512]{1,2,0:T(8,128)}, f32[24,128,512]{1,2,0:T(8,128)}, u32[]{:S(2)}, u32[]{:S(2)}) collective-permute-start(f32[24,128,512]{1,2,0:T(8,128)} %copy.8), channel_id=1, source_target_pairs={{0,16},{1,17},{2,18},{3,19},{4,20},{5,21},{6,22},{7,23},{8,24},{9,... | collective-permute-start | bytes 18874376 | tf_op jit(solution)/shard_map/ppermute | solution.py:12
  783.7 65.9 %collective-permute-start.15 = (f32[12,128,512]{1,2,0:T(8,128)S(1)}, f32[12,128,512]{1,2,0:T(8,128)S(1)}, u32[]{:S(2)}, u32[]{:S(2)}) collective-permute-start(f32[12,128,512]{1,2,0:T(8,128)S(1)} %slice.145), channel_id=1, source_target_pairs={{0,32},{1,33},{2,34},{3,35},{4,36},{5,37},{6,38},{7,39},{8,40},{9,... | collective-permute-start | bytes 9437192 | tf_op jit(solution)/shard_map/ppermute | solution.py:12
  850.3 34.3 %collective-permute-start.16 = (f32[6,128,512]{1,2,0:T(8,128)S(1)}, f32[6,128,512]{1,2,0:T(8,128)S(1)}, u32[]{:S(2)}, u32[]{:S(2)}) collective-permute-start(f32[6,128,512]{1,2,0:T(8,128)S(1)} %slice.147), channel_id=1, source_target_pairs={{0,64},{1,65},{2,66},{3,67},{4,68},{5,69},{6,70},{7,71},{8,72},{9,... | collective-permute-start | bytes 4718600 | tf_op jit(solution)/shard_map/ppermute | solution.py:12
where the time goes:
time: 898 us; the launch traced here: 887 us
  waiting for transfers between devices  599 us (67%)
  matrix products  109 us (12%)
  local copies, waits for them, and re-layouts  100 us (11%)
  other arithmetic  46.9 us (5%)
  starting transfers between devices  30.9 us (3%)
    ppermute x17, waiting for transfers between devices, partner(): return lax.ppermute(value, axis, pairs)  599 us
    dot_general x6, matrix products, local(): jnp.dot(blocks[slot_num], stacked, precision=HIGHEST, preferred_element_t...  92.9 us
    gather x6, local copies, waits for them, and re-layouts, local(): features[col_ids[slot_num]].reshape(per_row * tile_rows, feat_width)  39.2 us
    unnamed x34, local copies, waits for them, and re-layouts  36.1 us
    ppermute x17, starting transfers between devices, partner(): return lax.ppermute(value, axis, pairs)  30.9 us
  transfers between devices with their start and end apart: 17, of which 14 were waited for; matrix products, arithmetic and copies ran while one was open for 2% of the time, Pallas kernels for 0%

commit v1 on v0

v1 whole, which is shorter than its diff:
```python
import functools

import jax
import jax.numpy as jnp
from jax import lax
from jax.experimental import pallas as pl
from jax.experimental.pallas import tpu as pltpu
from jax.sharding import PartitionSpec as P

MESH = pl.DeviceIdType.MESH
F32 = jnp.float32
BF16 = jnp.bfloat16
I32 = jnp.int32

B = 128
FEAT = 512
SLOTS = 6
BPR = 32
FT = 16
HALF = B // 2
LANES = 128
GROUPS = FEAT // LANES
TILE_ROWS = HALF * GROUPS
SHIFT = {"z": 5, "y": 3, "x": 1}
PIECES = ((88, 0, "zyx"), (88, 88, "yxz"), (80, 176, "xzy"))


def split(value):
    high = value.astype(BF16)
    return high, (value - high.astype(F32)).astype(BF16)


def product(left_high, left_low, right_high, right_low):
    dot = functools.partial(jnp.dot, preferred_element_type=F32)
    return dot(left_high, right_high) + (dot(left_high, right_low) + dot(left_low, right_high))


def product_kernel(col_ids, row_ids, blocks, features, part, labels, total, f_high, f_low, a_high, a_low):
    k = pl.program_id(0)

    @pl.when(k == 0)
    def _():
        for t in range(FT):
            high, low = split(features[t])
            f_high[pl.ds(t * B, B), :] = high
            f_low[pl.ds(t * B, B), :] = low
        row = lax.broadcasted_iota(I32, (8, LANES), 0)
        tile = jnp.full((8, LANES), -1, I32)
        for s in range(SLOTS):
            tile = jnp.where(row == s, row_ids[s], tile)
        labels[...] = tile

    total[...] = jnp.zeros_like(total)
    for j in range(BPR):
        t = col_ids[k, j]
        total[t] += blocks[0, :, pl.ds(j * B, B)]
    for t in range(FT):
        high, low = split(total[t])
        a_high[:, pl.ds(t * B, B)] = high
        a_low[:, pl.ds(t * B, B)] = low
    result = product(a_high[...], a_low[...], f_high[...], f_low[...])
    for half in range(2):
        for g in range(GROUPS):
            part[half, 0, pl.ds(g * HALF, HALF), :] = result[
                half * HALF : (half + 1) * HALF, g * LANES : (g + 1) * LANES
            ]


def local_product(blocks, features, col_ids, row_ids):
    return pl.pallas_call(
        product_kernel,
        grid_spec=pltpu.PrefetchScalarGridSpec(
            num_scalar_prefetch=2,
            grid=(SLOTS,),
            in_specs=[
                pl.BlockSpec((1, B, BPR * B), lambda k, *_: (k, 0, 0)),
                pl.BlockSpec((FT, B, FEAT), lambda k, *_: (0, 0, 0), pipeline_mode=pl.Buffered(1)),
            ],
            out_specs=[
                pl.BlockSpec((2, 1, TILE_ROWS, LANES), lambda k, *_: (0, k, 0, 0)),
                pl.BlockSpec((8, LANES), lambda k, *_: (0, 0)),
            ],
            scratch_shapes=[
                pltpu.VMEM((FT, B, B), F32),
                pltpu.VMEM((FT * B, FEAT), BF16),
                pltpu.VMEM((FT * B, FEAT), BF16),
                pltpu.VMEM((B, FT * B), BF16),
                pltpu.VMEM((B, FT * B), BF16),
            ],
        ),
        out_shape=[
            jax.ShapeDtypeStruct((2, SLOTS, TILE_ROWS, LANES), F32),
            jax.ShapeDtypeStruct((8, LANES), I32),
        ],
        compiler_params=pltpu.CompilerParams(vmem_limit_bytes=48 << 20),
    )(col_ids, row_ids, blocks, features)


PIECE_BUFFERS = (
    ("entries", 64),
    ("sums", 65),
    ("a2_far_up", 4),
    ("a2_far_down", 4),
    ("a2_got_far_up", 4),
    ("a2_got_far_down", 4),
    ("a2_up", 8),
    ("a2_down", 8),
    ("a2_got_up", 8),
    ("a2_got_down", 8),
    ("quarter", 8),
    ("a3_got_far_up", 1),
    ("a3_got_far_down", 1),
    ("a3_up", 1),
    ("a3_down", 1),
    ("a3_got_up", 2),
    ("a3_got_down", 2),
    ("dense", 33),
    ("b1_far_up", 6),
    ("b1_far_down", 6),
    ("b1_got_far_up", 6),
    ("b1_got_far_down", 6),
    ("b1_up", 12),
    ("b1_down", 12),
    ("b1_got_up", 12),
    ("b1_got_down", 12),
    ("answers", 12),
)
N_PIECES = len(PIECES)
N_SEMS = 64 * N_PIECES
N_LOCAL = 16 * N_PIECES


class Piece:
    pass


def exchange_kernel(part, labels, factor, owned, returned, *scratch):
    scratch = list(scratch)
    pieces = []
    for number, (rows, start, order) in enumerate(PIECES):
        piece = Piece()
        piece.number, piece.rows, piece.start, piece.order = number, rows, start, order
        for name, _ in PIECE_BUFFERS:
            setattr(piece, name, scratch.pop(0))
        pieces.append(piece)
    lab, tab_v, tab, x_buf, y_buf, fac, fac_high, fac_low, send_sem, recv_sem, local_sem = scratch

    z = lax.axis_index("gx")
    gy = lax.axis_index("gy")
    core = gy % 2
    at = {"z": z, "y": gy // 8, "x": (gy // 2) % 4}

    def neighbour(axis, step):
        to = dict(at)
        to[axis] = (at[axis] + step) % 4
        return (to["z"], to["y"] * 8 + to["x"] * 2 + core)

    sibling = (z, gy - core + (1 - core))
    counts = {"remote": 0, "local": 0}
    sent = []

    def remote(source, target, device):
        n = counts["remote"]
        counts["remote"] += 1
        copy = pltpu.make_async_remote_copy(
            src_ref=source,
            dst_ref=target,
            send_sem=send_sem.at[n],
            recv_sem=recv_sem.at[n],
            device_id=device,
            device_id_type=MESH,
        )
        copy.start()
        sent.append(copy)
        return copy

    def local(source, target):
        n = counts["local"]
        counts["local"] += 1
        copy = pltpu.make_async_copy(source, target, local_sem.at[n])
        copy.start()
        return copy

    barrier = pltpu.get_barrier_semaphore()
    greeted = [sibling] + [neighbour(axis, step) for axis in "zyx" for step in (1, 3)]
    for device in greeted:
        pl.semaphore_signal(barrier, inc=1, device_id=device, device_id_type=MESH)
    own_labels = local(labels, lab.at[0, pl.ds(0, 8)])
    get_factor = local(factor, fac)
    for p in pieces:
        p.own = local(part.at[core, :, pl.ds(p.start, p.rows), :], p.entries.at[pl.ds(0, SLOTS)])
        p.sums[0] = jnp.zeros((p.rows, LANES), F32)
        p.dense[0] = jnp.zeros((p.rows, LANES), F32)
    pl.semaphore_wait(barrier, len(greeted))

    sibling_labels = remote(labels, lab.at[0, pl.ds(8, 8)], sibling)
    for p in pieces:
        p.other = remote(
            part.at[1 - core, :, pl.ds(p.start, p.rows), :], p.entries.at[pl.ds(8, SLOTS)], sibling
        )
    for p in pieces:
        p.up, p.down = neighbour(p.order[0], 1), neighbour(p.order[0], 3)
        p.list_up, p.list_down = {}, {}
        for turn in range(2):
            t_up, t_down = turn, 1 - turn
            p.list_up[0, t_up] = remote(
                part.at[core, pl.ds(3 * t_up, 3), pl.ds(p.start, p.rows), :],
                p.entries.at[pl.ds(16 + 3 * t_up, 3)],
                p.up,
            )
            p.list_down[0, t_down] = remote(
                part.at[core, pl.ds(3 * t_down, 3), pl.ds(p.start, p.rows), :],
                p.entries.at[pl.ds(32 + 3 * t_down, 3)],
                p.down,
            )
    own_labels.wait()
    sibling_labels.wait_recv()
    for p in pieces:
        j = p.number
        p.lab_up = remote(lab.at[0], lab.at[1 + 3 * j], p.up)
        p.lab_down = remote(lab.at[0], lab.at[2 + 3 * j], p.down)
    for p in pieces:
        p.other.wait_recv()
        for turn in range(2):
            t_up, t_down = turn, 1 - turn
            p.list_up[1, t_up] = remote(
                p.entries.at[pl.ds(8 + 3 * t_up, 3)], p.entries.at[pl.ds(24 + 3 * t_up, 3)], p.up
            )
            p.list_down[1, t_down] = remote(
                p.entries.at[pl.ds(8 + 3 * t_down, 3)], p.entries.at[pl.ds(40 + 3 * t_down, 3)], p.down
            )
    for p in pieces:
        p.lab_up.wait_recv()
        p.lab_far = remote(lab.at[1 + 3 * p.number], lab.at[3 + 3 * p.number], p.up)
    get_factor.wait()
    high, low = split(fac[...])
    fac_high[...] = high
    fac_low[...] = low
    for p in pieces:
        p.lab_down.wait_recv()
        p.lab_far.wait_recv()
        j = p.number
        first, second, third = p.order
        seen = jnp.concatenate([lab[0], lab[1 + 3 * j], lab[2 + 3 * j], lab[3 + 3 * j]], axis=0)
        row = lax.broadcasted_iota(I32, (64, LANES), 0)
        lane = lax.broadcasted_iota(I32, (64, LANES), 1)
        wanted = jnp.sum(jnp.where(row == lane, seen, 0), axis=0, keepdims=True)
        previous = jnp.max(
            jnp.where(jnp.logical_and(seen == wanted, row < lane), row + 1, 0), axis=0, keepdims=True
        )

        def step_of(order):
            return jnp.where(order == 1, 3, jnp.where(order == 2, 1, jnp.where(order == 3, 2, 0)))

        def order_of(step):
            return jnp.where(step == 0, 0, jnp.where(step == 3, 1, step + 1))

        named = (
            (at[first] << SHIFT[first])
            + (((at[second] + step_of((lane >> 3) & 3)) & 3) << SHIFT[second])
            + (((at[third] + step_of((lane >> 1) & 3)) & 3) << SHIFT[third])
            + (lane & 1)
        )
        last = jnp.max(jnp.where(seen == named, row + 1, 0), axis=0, keepdims=True)
        place = (
            1
            + order_of((((wanted >> SHIFT[second]) & 3) - at[second]) & 3) * 8
            + order_of((((wanted >> SHIFT[third]) & 3) - at[third]) & 3) * 2
            + (wanted & 1)
        )
        place = jnp.where(((wanted >> SHIFT[first]) & 3) == at[first], place, 0)
        line = lax.broadcasted_iota(I32, (8, LANES), 0)
        tab_v[j] = jnp.where(line == 0, previous, jnp.where(line == 1, last, place))
    for p in pieces:
        p.far_up, p.far_down = {}, {}
        for h in range(2):
            p.list_up[h, 0].wait_recv()
            p.far_up[h] = remote(
                p.entries.at[pl.ds(16 + 8 * h, 3)], p.entries.at[pl.ds(48 + 8 * h, 3)], p.up
            )
            p.list_down[h, 1].wait_recv()
            p.far_down[h] = remote(
                p.entries.at[pl.ds(35 + 8 * h, 3)], p.entries.at[pl.ds(51 + 8 * h, 3)], p.down
            )
    get_tab = local(tab_v, tab)
    get_tab.wait()

    def add_lists(p, order):
        def body(h, carry):
            for s in range(SLOTS):
                i = order * 16 + h * 8 + s
                p.sums[i + 1] = p.entries[i] + p.sums[tab[p.number, 0, i]]
            return carry

        lax.fori_loop(0, 2, body, 0)

    for p in pieces:
        p.own.wait()
        add_lists(p, 0)
    for p in pieces:
        p.list_up[0, 1].wait_recv()
        p.list_up[1, 1].wait_recv()
        add_lists(p, 1)
        p.list_down[0, 0].wait_recv()
        p.list_down[1, 0].wait_recv()
        add_lists(p, 2)

    def pick(p, r):
        return p.sums[tab[p.number, 1, r]]

    for p in pieces:
        for h in range(2):
            p.far_up[h].wait_recv()
            p.far_down[h].wait_recv()
        add_lists(p, 3)
        p.up, p.down = neighbour(p.order[1], 1), neighbour(p.order[1], 3)

        def far_body(m, carry, p=p):
            p.a2_far_up[m] = pick(p, 24 + m)
            p.a2_far_down[m] = pick(p, 28 + m)
            return carry

        lax.fori_loop(0, 4, far_body, 0)

        def near_body(m, carry, p=p):
            p.a2_up[m + 4] = pick(p, 20 + m)
            p.a2_down[m] = pick(p, 8 + m)
            return carry

        lax.fori_loop(0, 4, near_body, 0)
        p.a2_far = (
            remote(p.a2_far_up, p.a2_got_far_up, p.up),
            remote(p.a2_far_down, p.a2_got_far_down, p.down),
        )
        p.a2_near = [
            remote(p.a2_up.at[pl.ds(4, 4)], p.a2_got_up.at[pl.ds(4, 4)], p.up),
            remote(p.a2_down.at[pl.ds(0, 4)], p.a2_got_down.at[pl.ds(0, 4)], p.down),
        ]
    for p in pieces:
        p.a2_far[0].wait_recv()

        def up_body(m, carry, p=p):
            p.a2_up[m] = p.a2_got_far_up[m] + pick(p, 16 + m)
            return carry

        lax.fori_loop(0, 4, up_body, 0)
        p.a2_near.append(remote(p.a2_up.at[pl.ds(0, 4)], p.a2_got_up.at[pl.ds(0, 4)], p.up))
        p.a2_far[1].wait_recv()

        def down_body(m, carry, p=p):
            p.a2_down[m + 4] = p.a2_got_far_down[m] + pick(p, 12 + m)
            return carry

        lax.fori_loop(0, 4, down_body, 0)
        p.a2_near.append(remote(p.a2_down.at[pl.ds(4, 4)], p.a2_got_down.at[pl.ds(4, 4)], p.down))

    for p in pieces:
        for copy in p.a2_near:
            copy.wait_recv()

        def quarter_body(m, carry, p=p):
            p.quarter[m] = pick(p, m) + (p.a2_got_up[m] + p.a2_got_down[m])
            return carry

        lax.fori_loop(0, 8, quarter_body, 0)
        p.up, p.down = neighbour(p.order[2], 1), neighbour(p.order[2], 3)
        p.a3_far = (
            remote(p.quarter.at[6], p.a3_got_far_up.at[0], p.up),
            remote(p.quarter.at[7], p.a3_got_far_down.at[0], p.down),
        )
        p.a3_near = [
            remote(p.quarter.at[5], p.a3_got_up.at[1], p.up),
            remote(p.quarter.at[2], p.a3_got_down.at[0], p.down),
        ]
    for p in pieces:
        p.a3_far[0].wait_recv()
        p.a3_up[0] = p.quarter[4] + p.a3_got_far_up[0]
        p.a3_far[1].wait_recv()
        p.a3_down[0] = p.quarter[3] + p.a3_got_far_down[0]
        p.a3_near.append(remote(p.a3_up.at[0], p.a3_got_up.at[0], p.up))
        p.a3_near.append(remote(p.a3_down.at[0], p.a3_got_down.at[1], p.down))
    for p in pieces:
        for copy in p.a3_near:
            copy.wait_recv()
        for b in range(2):
            x_buf[b, pl.ds(p.start, p.rows), :] = jnp.tanh(
                p.quarter[b] + (p.a3_got_up[b] + p.a3_got_down[b])
            )

    x = jnp.concatenate(
        [
            jnp.concatenate([x_buf[b, pl.ds(g * HALF, HALF), :] for g in range(GROUPS)], axis=1)
            for b in range(2)
        ],
        axis=0,
    )
    x_high, x_low = split(x)
    y = product(x_high, x_low, fac_high[...], fac_low[...])
    for b in range(2):
        rows_y = y[b * HALF : (b + 1) * HALF]
        y_buf[b] = rows_y
        flat = jnp.concatenate([rows_y[:, g * LANES : (g + 1) * LANES] for g in range(GROUPS)], axis=0)
        for p in pieces:
            p.dense[1 + b] = flat[p.start : p.start + p.rows]

    for p in pieces:
        d = p.dense
        p.b3 = {}
        p.b3["up", 0] = remote(d.at[1], d.at[3], p.up)
        p.b3["down", 1] = remote(d.at[2], d.at[6], p.down)
        p.b3["up", 1] = remote(d.at[2], d.at[4], p.up)
        p.b3["down", 0] = remote(d.at[1], d.at[5], p.down)
    half_rows = pl.ds(pl.multiple_of(core * HALF, HALF), HALF)
    keep = local(y_buf.at[core], owned.at[half_rows, :])
    give = remote(y_buf.at[1 - core], owned.at[half_rows, :], sibling)
    for p in pieces:
        d = p.dense
        p.b3["up", 0].wait_recv()
        p.b3["far", 0] = remote(d.at[3], d.at[7], p.up)
        p.b3["down", 1].wait_recv()
        p.b3["far", 1] = remote(d.at[6], d.at[8], p.down)
    for p in pieces:
        d = p.dense
        for key in (("up", 1), ("down", 0), ("far", 0), ("far", 1)):
            p.b3[key].wait_recv()
        p.up, p.down = neighbour(p.order[1], 1), neighbour(p.order[1], 3)
        p.b2 = {}
        p.b2["up", 0] = remote(d.at[pl.ds(1, 4)], d.at[pl.ds(9, 4)], p.up)
        p.b2["down", 1] = remote(d.at[pl.ds(5, 4)], d.at[pl.ds(21, 4)], p.down)
        p.b2["up", 1] = remote(d.at[pl.ds(5, 4)], d.at[pl.ds(13, 4)], p.up)
        p.b2["down", 0] = remote(d.at[pl.ds(1, 4)], d.at[pl.ds(17, 4)], p.down)
    for p in pieces:
        d = p.dense
        p.b2["up", 0].wait_recv()
        p.b2["far", 0] = remote(d.at[pl.ds(9, 4)], d.at[pl.ds(25, 4)], p.up)
        p.b2["down", 1].wait_recv()
        p.b2["far", 1] = remote(d.at[pl.ds(21, 4)], d.at[pl.ds(29, 4)], p.down)

    def answer(p, i):
        return p.dense[tab[p.number, 2, i]]

    for p in pieces:
        for key in (("up", 1), ("down", 0), ("far", 0), ("far", 1)):
            p.b2[key].wait_recv()
        p.up, p.down = neighbour(p.order[0], 1), neighbour(p.order[0], 3)

        def far_body(h, carry, p=p):
            for s in range(3):
                p.b1_far_up[h * 3 + s] = answer(p, 48 + h * 8 + s)
                p.b1_far_down[h * 3 + s] = answer(p, 51 + h * 8 + s)
            return carry

        lax.fori_loop(0, 2, far_body, 0)
        p.b1_far = (
            remote(p.b1_far_up, p.b1_got_far_up, p.up),
            remote(p.b1_far_down, p.b1_got_far_down, p.down),
        )

        def near_body(h, carry, p=p):
            for s in range(3):
                p.b1_up[6 + h * 3 + s] = answer(p, 35 + h * 8 + s)
                p.b1_down[h * 3 + s] = answer(p, 16 + h * 8 + s)
            return carry

        lax.fori_loop(0, 2, near_body, 0)
        p.b1_near = [
            remote(p.b1_up.at[pl.ds(6, 6)], p.b1_got_up.at[pl.ds(6, 6)], p.up),
            remote(p.b1_down.at[pl.ds(0, 6)], p.b1_got_down.at[pl.ds(0, 6)], p.down),
        ]
    for p in pieces:
        p.b1_far[0].wait_recv()

        def up_body(h, carry, p=p):
            for s in range(3):
                p.b1_up[h * 3 + s] = p.b1_got_far_up[h * 3 + s] + answer(p, 32 + h * 8 + s)
            return carry

        lax.fori_loop(0, 2, up_body, 0)
        p.b1_near.append(remote(p.b1_up.at[pl.ds(0, 6)], p.b1_got_up.at[pl.ds(0, 6)], p.up))
        p.b1_far[1].wait_recv()

        def down_body(h, carry, p=p):
            for s in range(3):
                p.b1_down[6 + h * 3 + s] = p.b1_got_far_down[h * 3 + s] + answer(p, 19 + h * 8 + s)
            return carry

        lax.fori_loop(0, 2, down_body, 0)
        p.b1_near.append(remote(p.b1_down.at[pl.ds(6, 6)], p.b1_got_down.at[pl.ds(6, 6)], p.down))
    last_local, last_remote = [], []
    for p in pieces:
        for copy in p.b1_near:
            copy.wait_recv()

        def answer_body(h, carry, p=p):
            for t in range(2):
                for s in range(3):
                    q = t * 6 + h * 3 + s
                    p.answers[h * 6 + t * 3 + s] = answer(p, h * 8 + t * 3 + s) + (
                        p.b1_got_up[q] + p.b1_got_down[q]
                    )
            return carry

        lax.fori_loop(0, 2, answer_body, 0)
        first_row = p.start
        while first_row < p.start + p.rows:
            g, r = divmod(first_row, HALF)
            n = min(HALF - r, p.start + p.rows - first_row)
            target = returned.at[
                :, pl.ds(pl.multiple_of(core * HALF + r, 8), n), pl.ds(g * LANES, LANES)
            ]
            here = pl.ds(first_row - p.start, n)
            last_remote.append(remote(p.answers.at[pl.ds(6, 6), here, :], target, sibling))
            last_local.append(local(p.answers.at[pl.ds(0, 6), here, :], target))
            first_row += n
    keep.wait()
    give.wait_recv()
    for copy in last_local:
        copy.wait()
    for copy in last_remote:
        copy.wait_recv()
    for copy in sent:
        copy.wait_send()


def exchange(part, labels, factor):
    scratch = []
    for rows, _, _ in PIECES:
        for _, depth in PIECE_BUFFERS:
            scratch.append(pltpu.VMEM((depth, rows, LANES), F32))
    scratch += [
        pltpu.VMEM((1 + 3 * N_PIECES, 16, LANES), I32),
        pltpu.VMEM((N_PIECES, 8, LANES), I32),
        pltpu.SMEM((N_PIECES, 8, LANES), I32),
        pltpu.VMEM((2, TILE_ROWS, LANES), F32),
        pltpu.VMEM((2, HALF, FEAT), F32),
        pltpu.VMEM((FEAT, FEAT), F32),
        pltpu.VMEM((FEAT, FEAT), BF16),
        pltpu.VMEM((FEAT, FEAT), BF16),
        pltpu.SemaphoreType.DMA((N_SEMS,)),
        pltpu.SemaphoreType.DMA((N_SEMS,)),
        pltpu.SemaphoreType.DMA((N_LOCAL,)),
    ]
    hbm = pl.BlockSpec(memory_space=pl.ANY)
    return pl.pallas_call(
        exchange_kernel,
        in_specs=[hbm] * 3,
        out_specs=[hbm] * 2,
        out_shape=[
            jax.ShapeDtypeStruct((B, FEAT), F32),
            jax.ShapeDtypeStruct((SLOTS, B, FEAT), F32),
        ],
        scratch_shapes=scratch,
        compiler_params=pltpu.CompilerParams(
            collective_id=0, has_side_effects=True, vmem_limit_bytes=60 << 20
        ),
    )(part, labels, factor)


def local_step(blocks, features, col_ids, row_ids, factor):
    part, labels = local_product(blocks, features, col_ids, row_ids)
    owned, returned = exchange(part, labels, factor)
    return owned, returned.reshape(SLOTS * B, FEAT)


def solution(mesh):
    return jax.shard_map(
        local_step,
        mesh=mesh,
        in_specs=(
            P(("gx", "gy"), None, None),
            P(("gx", "gy"), None, None),
            P(("gx", "gy"), None),
            P(("gx", "gy")),
            P(),
        ),
        out_specs=(P(("gx", "gy"), None), P(("gx", "gy"), None)),
        check_vma=False,
    )
```

time: 898 us -> 113 us (0.13); the launches traced: 887 us -> 113 us
  waiting for transfers between devices: 599 us -> 0 us
  matrix products: 109 us -> 0 us
  Pallas kernels: 0 us -> 103 us
  local copies, waits for them, and re-layouts: 100 us -> 9.59 us
  other arithmetic: 46.9 us -> 0 us
  starting transfers between devices: 30.9 us -> 0 us
    ppermute x17 -> x0, waiting for transfers between devices: 599 us -> none  [partner(): return lax.ppermute(value, axis, pairs)]
    dot_general x9 -> x0, matrix products: 109 us -> none  [the longest x6 92.9 us: local(): jnp.dot(blocks[slot_num], stacked, precision=HIGHEST, preferred_element_t...]
    pallas_call x0 -> x2, Pallas kernels: none -> 103 us  [the longest x1 90.9 us: exchange(): pl.pallas_call(exchange_kernel, in_specs=[hbm] * 3, out_specs=[hbm] * 2,...]
    gather x6 -> x0, local copies, waits for them, and re-layouts: 39.2 us -> none  [local(): features[col_ids[slot_num]].reshape(per_row * tile_rows, feat_width)]
    ppermute x17 -> x0, starting transfers between devices: 30.9 us -> none  [partner(): return lax.ppermute(value, axis, pairs)]
    select_n x20 -> x0, other arithmetic: 29.4 us -> none  [the longest x3 15.3 us: local(): jnp.where(kept_mask[:, None, None], values, 0.0)]
    unnamed x34 -> x12, local copies, waits for them, and re-layouts: 36.1 us -> 9.59 us
    slice x5 -> x0, local copies, waits for them, and re-layouts: 23.4 us -> none  [the longest x4 16.8 us: local(): incoming = partner(answers[count_kept:], ('gx', 'gy'), record[3])]
  transfers between devices with their start and end apart: 17 -> 0, of which waited for: 14 -> 0; matrix products, arithmetic and copies ran while one was open for 2% -> 0% of each run, Pallas kernels for 0% -> 0%
where the time goes in v1:
time: 113 us
  Pallas kernels  103 us (91%)
  local copies, waits for them, and re-layouts  9.59 us (8%)
    pallas_call x1, Pallas kernels, exchange(): pl.pallas_call(exchange_kernel, in_specs=[hbm] * 3, out_specs=[hbm] * 2,...  90.9 us
    pallas_call x1, Pallas kernels, local_product(): pl.pallas_call(product_kernel, grid_spec=pltpu.PrefetchScalarGridSpec(num...  11.6 us
    unnamed x12, local copies, waits for them, and re-layouts  9.59 us

profile of v1, /device:TPU:1, one launch (start us, length us, event | category | flops | bytes accessed | tf_op | source)
XLA Modules:
  0.0 112.8 jit_solution(337204246101022741)
XLA Ops:
  0.6 0.0 copy-start
  0.6 2.2 %copy-done = f32[16,128,512]{2,1,0:T(8,128)S(1)} copy-done((f32[16,128,512]{2,1,0:T(8,128)S(1)}, f32[16,128,512]{2,1,0:T(8,128)}, u32[]{:S(2)}) %copy-start) | copy-done | bytes 4194328
  2.8 0.0 copy-start.3
  2.8 0.7 copy-done.3
  3.5 0.0 copy-start.4
  3.5 0.7 copy-done.4
  4.2 11.6 %shard_map.68 = (f32[2,6,256,128]{3,2,1,0:T(8,128)S(1)}, s32[8,128]{1,0:T(8,128)S(1)}) custom-call(s32[6,32]{1,0:T(8,128)S(1)} %copy-done.3, s32[6]{0:T(128)S(1)} %copy-done.4, f32[6,128,4096]{2,1,0:T(8,128)} %blocks.1, f32[16,128,512]{2,1,0:T(8,128)S(1)} %copy-done), custom_call_target="tpu_custom_call" | custom-call | tf_op jit(solution)/shard_map/pallas_call | solution.py:70
  15.8 0.0 copy-start.1
  15.8 1.1 %copy-done.1 = f32[2,6,256,128]{3,2,1,0:T(8,128)} copy-done((f32[2,6,256,128]{3,2,1,0:T(8,128)}, f32[2,6,256,128]{3,2,1,0:T(8,128)S(1)}, u32[]{:S(2)}) %copy-start.1) | copy-done | bytes 1572888
  16.9 0.0 copy-start.2
  16.9 0.6 copy-done.2
  17.5 90.9 %shard_map.69 = (f32[128,512]{1,0:T(8,128)}, f32[6,128,512]{2,1,0:T(8,128)}) custom-call(f32[2,6,256,128]{3,2,1,0:T(8,128)} %copy-done.1, s32[8,128]{1,0:T(8,128)} %copy-done.2, f32[512,512]{1,0:T(8,128)} %factor.1), custom_call_target="tpu_custom_call" | custom-call | tf_op jit(solution)/shard_map/pallas_call | solution.py:544
  108.5 1.7 %copy.9 = f32[128,512]{1,0:T(8,128)} copy(f32[128,512]{1,0:T(8,128)} %get-tuple-element.12) | data formatting | bytes 524288
  110.1 2.7 %copy.10 = f32[768,512]{1,0:T(8,128)} copy(f32[768,512]{1,0:T(8,128)} %bitcast.1) | data formatting | bytes 3145728
Async XLA Ops:
  0.6 2.2 %copy-start = (f32[16,128,512]{2,1,0:T(8,128)S(1)}, f32[16,128,512]{2,1,0:T(8,128)}, u32[]{:S(2)}) copy-start(f32[16,128,512]{2,1,0:T(8,128)} %features.1) | copy-start | bytes 12582916
  2.8 0.7 copy-start.3
  3.5 0.7 copy-start.4
  15.8 1.1 %copy-start.1 = (f32[2,6,256,128]{3,2,1,0:T(8,128)}, f32[2,6,256,128]{3,2,1,0:T(8,128)S(1)}, u32[]{:S(2)}) copy-start(f32[2,6,256,128]{3,2,1,0:T(8,128)S(1)} %get-tuple-element.6.part) | copy-start | bytes 4718596
  16.9 0.6 copy-start.2

commit v2 on v0

v2 whole, which is shorter than its diff:
```python
import functools

import jax
import jax.numpy as jnp
from jax import lax
from jax.experimental import pallas as pl
from jax.experimental.pallas import tpu as pltpu
from jax.sharding import PartitionSpec as P

MESH = pl.DeviceIdType.MESH
F32 = jnp.float32
BF16 = jnp.bfloat16
I32 = jnp.int32

B = 128
FEAT = 512
SLOTS = 6
BPR = 32
FT = 16
HALF = B // 2
STREAMS = 2
ROWS = HALF // STREAMS
LANES = 128
GROUPS = FEAT // LANES
TILE_ROWS = ROWS * GROUPS
SHIFT = {"z": 5, "y": 3, "x": 1}
ORDERS = ("zyx", "yxz", "xzy")
PIECES = (((0, 48), (48, 40), (88, 40)), ((0, 40), (40, 48), (88, 40)))
PAIRS = SLOTS // 2
FAR_UP = ((0, 0), (1, 0), (0, 1))
FAR_DOWN = ((1, 1), (0, 2), (1, 2))


def split(value):
    high = value.astype(BF16)
    return high, (value - high.astype(F32)).astype(BF16)


def product(left_high, left_low, right_high, right_low):
    dot = functools.partial(jnp.dot, preferred_element_type=F32)
    return dot(left_high, right_high) + (dot(left_high, right_low) + dot(left_low, right_high))


PIECE_BUFFERS = (
    ("sums", 49),
    ("a2_far_up", 4),
    ("a2_far_down", 4),
    ("a2_got_far_up", 4),
    ("a2_got_far_down", 4),
    ("a2_up", 8),
    ("a2_down", 8),
    ("a2_got_up", 8),
    ("a2_got_down", 8),
    ("quarter", 8),
    ("a3_got_far_up", 1),
    ("a3_got_far_down", 1),
    ("a3_up", 1),
    ("a3_down", 1),
    ("a3_got_up", 2),
    ("a3_got_down", 2),
    ("dense", 33),
    ("b1_far_up", 6),
    ("b1_far_down", 6),
    ("b1_got_far_up", 6),
    ("b1_got_far_down", 6),
    ("b1_up", 12),
    ("b1_down", 12),
    ("b1_got_up", 12),
    ("b1_got_down", 12),
)
N_REMOTE = 320
N_LOCAL = 32
RING = 4


class Piece:
    pass


def slot_place(pair, half):
    return half * SLOTS + 2 * pair


def kernel(blocks, features, col_ids, row_ids, factor, owned, returned, *scratch):
    scratch = list(scratch)
    streams = []
    for u in range(STREAMS):
        pieces = []
        for number, (start, rows) in enumerate(PIECES[u]):
            piece = Piece()
            piece.number, piece.start, piece.rows, piece.order = number, start, rows, ORDERS[number]
            piece.stream = u
            for name, _ in PIECE_BUFFERS:
                setattr(piece, name, scratch.pop(0))
            pieces.append(piece)
        streams.append(pieces)
    (
        blk, feat, f_high, f_low, chain, a_high, a_low, part, entries, cols, col_v, col_tab, ids,
        tile, lab, tab_v, tab, x_buf, y_buf, out_buf, fac, fac_high, fac_low,
        send_sem, recv_sem, local_sem,
    ) = scratch

    z = lax.axis_index("gx")
    gy = lax.axis_index("gy")
    core = gy % 2
    at = {"z": z, "y": gy // 8, "x": (gy // 2) % 4}

    def neighbour(axis, step):
        to = dict(at)
        to[axis] = (at[axis] + step) % 4
        return (to["z"], to["y"] * 8 + to["x"] * 2 + core)

    sibling = (z, gy - core + (1 - core))
    counts = {"remote": 0, "local": 0}
    sent = []

    def remote(source, target, device):
        n = counts["remote"]
        counts["remote"] += 1
        assert n < N_REMOTE
        copy = pltpu.make_async_remote_copy(
            src_ref=source,
            dst_ref=target,
            send_sem=send_sem.at[n],
            recv_sem=recv_sem.at[n],
            device_id=device,
            device_id_type=MESH,
        )
        copy.start()
        sent.append(copy)
        return copy

    def local(source, target):
        n = counts["local"]
        counts["local"] += 1
        assert n < N_LOCAL
        copy = pltpu.make_async_copy(source, target, local_sem.at[n])
        copy.start()
        return copy

    barrier = pltpu.get_barrier_semaphore()
    greeted = [sibling] + [neighbour(axis, step) for axis in "zyx" for step in (1, 3)]
    for device in greeted:
        pl.semaphore_signal(barrier, inc=1, device_id=device, device_id_type=MESH)
    get_cols = local(col_ids, cols)
    get_ids = local(row_ids, ids)
    get_feat = [local(features.at[pl.ds(4 * i, 4)], feat.at[pl.ds(4 * i, 4)]) for i in range(2)]
    get_blk = {k: local(blocks.at[k], blk.at[k % RING]) for k in range(2)}
    get_feat += [local(features.at[pl.ds(4 * i, 4)], feat.at[pl.ds(4 * i, 4)]) for i in range(2, 4)]
    for k in range(2, RING):
        get_blk[k] = local(blocks.at[k], blk.at[k % RING])
    get_factor = local(factor, fac)

    get_cols.wait()
    row = lax.broadcasted_iota(I32, (BPR, BPR), 0)
    lane = lax.broadcasted_iota(I32, (BPR, BPR), 1)
    for k in range(SLOTS):
        across = jnp.broadcast_to(cols[pl.ds(k, 1), :], (BPR, BPR))
        down = jnp.sum(jnp.where(row == lane, across, 0), axis=1, keepdims=True)
        col_v[pl.ds(2 * k, 1), pl.ds(0, BPR)] = jnp.max(
            jnp.where(jnp.logical_and(down == across, row < lane), row + 1, 0), axis=0, keepdims=True
        )
        col_v[pl.ds(2 * k + 1, 1), pl.ds(0, BPR)] = jnp.max(
            jnp.where(down == lane, row + 1, 0), axis=0, keepdims=True
        )
    get_ids.wait()
    line = lax.broadcasted_iota(I32, (8, LANES), 0)
    names = jnp.full((8, LANES), -1, I32)
    for s in range(SLOTS):
        names = jnp.where(line == s, ids[s], names)
    tile[...] = names
    chain[0] = jnp.zeros((B, B), F32)
    for pieces in streams:
        for p in pieces:
            p.sums[0] = jnp.zeros((p.rows, LANES), F32)
            p.dense[0] = jnp.zeros((p.rows, LANES), F32)

    def convert(first):
        def body(t, carry):
            high, low = split(feat[t])
            f_high[pl.ds(pl.multiple_of(t * B, B), B), :] = high
            f_low[pl.ds(pl.multiple_of(t * B, B), B), :] = low
            return carry

        lax.fori_loop(first, first + 4, body, 0)

    get_feat[0].wait()
    convert(0)
    get_col_tab = local(col_v, col_tab)
    get_feat[1].wait()
    convert(4)
    get_col_tab.wait()

    def gather_sums(k):
        get_blk[k].wait()
        held = blk.at[k % RING]

        for j in range(BPR):
            chain[j + 1] = held[:, pl.ds(j * B, B)] + chain[col_tab[2 * k, j]]
        for t in range(FT):
            high, low = split(chain[col_tab[2 * k + 1, t]])
            a_high[pl.ds((k % 2) * B, B), pl.ds(t * B, B)] = high
            a_low[pl.ds((k % 2) * B, B), pl.ds(t * B, B)] = low
        if k + RING < SLOTS:
            get_blk[k + RING] = local(blocks.at[k + RING], blk.at[k % RING])

    def multiply(pair):
        result = product(a_high[...], a_low[...], f_high[...], f_low[...])
        for s in range(2):
            for half in range(2):
                for u in range(STREAMS):
                    first = s * B + half * HALF + u * ROWS
                    for g in range(GROUPS):
                        part[2 * pair + s, half, u, pl.ds(g * ROWS, ROWS), :] = result[
                            first : first + ROWS, g * LANES : (g + 1) * LANES
                        ]

    give_part = {}

    def send_part(pair):
        give_part[pair] = remote(
            part.at[pl.ds(2 * pair, 2), 1 - core], entries.at[pl.ds(slot_place(pair, 1), 2)], sibling
        )

    def send_list(pieces, half, pair):
        for p in pieces:
            here = pl.ds(p.start, p.rows)
            if half == 0:
                source = part.at[pl.ds(2 * pair, 2), core, p.stream, here]
            else:
                source = entries.at[pl.ds(slot_place(pair, 1), 2), p.stream, here]
            for name, order, to in (("up", 1, 1), ("down", 2, 3)):
                target = entries.at[pl.ds(order * 12 + slot_place(pair, half), 2), p.stream, here]
                p.lists[name, half, pair] = remote(source, target, neighbour(p.order[0], to))

    def send_far(pieces, name, half, pair):
        order, to = (1, 1) if name == "up" else (2, 3)
        for p in pieces:
            here = pl.ds(p.start, p.rows)
            p.lists[name, half, pair].wait_recv()
            p.far[half, pair] = remote(
                entries.at[pl.ds(order * 12 + slot_place(pair, half), 2), p.stream, here],
                entries.at[pl.ds(36 + slot_place(pair, half), 2), p.stream, here],
                neighbour(p.order[0], to),
            )

    for pieces in streams:
        for p in pieces:
            p.lists, p.far = {}, {}
    first_stream, second_stream = streams

    gather_sums(0)
    pl.semaphore_wait(barrier, len(greeted))
    give_names = remote(tile, lab.at[0, pl.ds(8, 8)], sibling)
    keep_names = local(tile, lab.at[0, pl.ds(0, 8)])
    get_feat[2].wait()
    convert(8)
    get_feat[3].wait()
    convert(12)
    gather_sums(1)
    multiply(0)
    send_part(0)
    send_list(first_stream, 0, 0)
    send_list(second_stream, 0, 0)
    keep_names.wait()
    give_names.wait_recv()
    lab_up, lab_down, lab_far = {}, {}, {}
    for j in range(3):
        lab_up[j] = remote(lab.at[0], lab.at[1 + 3 * j], neighbour(ORDERS[j][0], 1))
        lab_down[j] = remote(lab.at[0], lab.at[2 + 3 * j], neighbour(ORDERS[j][0], 3))
    gather_sums(2)
    give_part[0].wait_recv()
    send_list(first_stream, 1, 0)
    send_list(second_stream, 1, 0)
    gather_sums(3)
    multiply(1)
    send_part(1)
    send_list(first_stream, 0, 1)
    send_list(second_stream, 0, 1)
    for j in range(3):
        lab_up[j].wait_recv()
        lab_far[j] = remote(lab.at[1 + 3 * j], lab.at[3 + 3 * j], neighbour(ORDERS[j][0], 1))
    gather_sums(4)
    give_part[1].wait_recv()
    send_list(first_stream, 1, 1)
    send_list(second_stream, 1, 1)
    gather_sums(5)
    multiply(2)
    send_part(2)
    send_list(first_stream, 0, 2)
    send_far(first_stream, "up", 0, 0)
    send_far(first_stream, "up", 1, 0)
    give_part[2].wait_recv()
    send_list(first_stream, 1, 2)
    send_list(second_stream, 0, 2)
    send_list(second_stream, 1, 2)

    def make_table(j):
        lab_down[j].wait_recv()
        lab_far[j].wait_recv()
        first, second, third = ORDERS[j]
        seen = jnp.concatenate([lab[0], lab[1 + 3 * j], lab[2 + 3 * j], lab[3 + 3 * j]], axis=0)
        row = lax.broadcasted_iota(I32, (64, LANES), 0)
        lane = lax.broadcasted_iota(I32, (64, LANES), 1)
        place_of_row = (row >> 4) * 12 + ((row >> 3) & 1) * 6 + (row & 7) + 1
        wanted = jnp.sum(jnp.where(row == lane, seen, 0), axis=0, keepdims=True)
        previous = jnp.max(
            jnp.where(jnp.logical_and(seen == wanted, row < lane), place_of_row, 0),
            axis=0,
            keepdims=True,
        )

        def step_of(order):
            return jnp.where(order == 1, 3, jnp.where(order == 2, 1, jnp.where(order == 3, 2, 0)))

        def order_of(step):
            return jnp.where(step == 0, 0, jnp.where(step == 3, 1, step + 1))

        named = (
            (at[first] << SHIFT[first])
            + (((at[second] + step_of((lane >> 3) & 3)) & 3) << SHIFT[second])
            + (((at[third] + step_of((lane >> 1) & 3)) & 3) << SHIFT[third])
            + (lane & 1)
        )
        last = jnp.max(jnp.where(seen == named, place_of_row, 0), axis=0, keepdims=True)
        place = (
            1
            + order_of((((wanted >> SHIFT[second]) & 3) - at[second]) & 3) * 8
            + order_of((((wanted >> SHIFT[third]) & 3) - at[third]) & 3) * 2
            + (wanted & 1)
        )
        place = jnp.where(((wanted >> SHIFT[first]) & 3) == at[first], place, 0)
        tab_v[j] = jnp.where(line == 0, previous, jnp.where(line == 1, last, place))

    for j in range(3):
        make_table(j)
    send_far(first_stream, "up", 0, 1)
    send_far(first_stream, "down", 1, 1)
    get_tab = local(tab_v, tab)
    send_far(first_stream, "down", 0, 2)
    send_far(second_stream, "up", 0, 0)
    send_far(second_stream, "up", 1, 0)
    send_far(first_stream, "down", 1, 2)
    get_tab.wait()

    def add_lists(pieces, order):
        for p in pieces:
            here = pl.ds(p.start, p.rows)
            for h in range(2):
                for s in range(SLOTS):
                    place = order * 12 + h * 6 + s
                    if order == 0 and h == 0:
                        value = part[s, core, p.stream, here]
                    else:
                        value = entries[place, p.stream, here]
                    p.sums[place + 1] = value + p.sums[tab[p.number, 0, order * 16 + h * 8 + s]]

    def add_near_lists(pieces):
        add_lists(pieces, 0)
        for p in pieces:
            for half in range(2):
                for pair in range(PAIRS):
                    if (half, pair) not in FAR_UP:
                        p.lists["up", half, pair].wait_recv()
                    if (half, pair) not in FAR_DOWN:
                        p.lists["down", half, pair].wait_recv()
        add_lists(pieces, 1)
        add_lists(pieces, 2)

    def pick(p, r):
        return p.sums[tab[p.number, 1, r]]

    def loop(n, body):
        def step(m, carry):
            body(m)
            return carry

        lax.fori_loop(0, n, step, 0)

    def a2_far(pieces):
        for p in pieces:
            for chunk in FAR_UP + FAR_DOWN:
                p.far[chunk].wait_recv()
            add_lists([p], 3)
            p.up, p.down = neighbour(p.order[1], 1), neighbour(p.order[1], 3)

            def body(m, p=p):
                p.a2_far_up[m] = pick(p, 24 + m)
                p.a2_far_down[m] = pick(p, 28 + m)

            loop(4, body)
            p.a2_far = (
                remote(p.a2_far_up, p.a2_got_far_up, p.up),
                remote(p.a2_far_down, p.a2_got_far_down, p.down),
            )

    def a2_near(pieces):
        for p in pieces:

            def body(m, p=p):
                p.a2_up[m + 4] = pick(p, 20 + m)
                p.a2_down[m] = pick(p, 8 + m)

            loop(4, body)
            p.a2_near = [
                remote(p.a2_up.at[pl.ds(4, 4)], p.a2_got_up.at[pl.ds(4, 4)], p.up),
                remote(p.a2_down.at[pl.ds(0, 4)], p.a2_got_down.at[pl.ds(0, 4)], p.down),
            ]

    def a2_merge(pieces):
        for p in pieces:
            p.a2_far[0].wait_recv()

            def up_body(m, p=p):
                p.a2_up[m] = p.a2_got_far_up[m] + pick(p, 16 + m)

            loop(4, up_body)
            p.a2_near.append(remote(p.a2_up.at[pl.ds(0, 4)], p.a2_got_up.at[pl.ds(0, 4)], p.up))
            p.a2_far[1].wait_recv()

            def down_body(m, p=p):
                p.a2_down[m + 4] = p.a2_got_far_down[m] + pick(p, 12 + m)

            loop(4, down_body)
            p.a2_near.append(
                remote(p.a2_down.at[pl.ds(4, 4)], p.a2_got_down.at[pl.ds(4, 4)], p.down)
            )

    def a3_start(pieces):
        for p in pieces:
            for copy in p.a2_near:
                copy.wait_recv()

            def body(m, p=p):
                p.quarter[m] = pick(p, m) + (p.a2_got_up[m] + p.a2_got_down[m])

            loop(8, body)
            p.up, p.down = neighbour(p.order[2], 1), neighbour(p.order[2], 3)
            p.a3_far = (
                remote(p.quarter.at[6], p.a3_got_far_up.at[0], p.up),
                remote(p.quarter.at[7], p.a3_got_far_down.at[0], p.down),
            )
            p.a3_near = [
                remote(p.quarter.at[5], p.a3_got_up.at[1], p.up),
                remote(p.quarter.at[2], p.a3_got_down.at[0], p.down),
            ]

    def a3_merge(pieces):
        for p in pieces:
            p.a3_far[0].wait_recv()
            p.a3_up[0] = p.quarter[4] + p.a3_got_far_up[0]
            p.a3_far[1].wait_recv()
            p.a3_down[0] = p.quarter[3] + p.a3_got_far_down[0]
            p.a3_near.append(remote(p.a3_up.at[0], p.a3_got_up.at[0], p.up))
            p.a3_near.append(remote(p.a3_down.at[0], p.a3_got_down.at[1], p.down))

    def a3_end(pieces):
        for p in pieces:
            for copy in p.a3_near:
                copy.wait_recv()
            for b in range(2):
                x_buf[p.stream, b, pl.ds(p.start, p.rows), :] = jnp.tanh(
                    p.quarter[b] + (p.a3_got_up[b] + p.a3_got_down[b])
                )

    give_owned, last_local = [], []

    def update(pieces):
        u = pieces[0].stream
        x = jnp.concatenate(
            [
                jnp.concatenate(
                    [x_buf[u, b, pl.ds(g * ROWS, ROWS), :] for g in range(GROUPS)], axis=1
                )
                for b in range(2)
            ],
            axis=0,
        )
        x_high, x_low = split(x)
        y = product(x_high, x_low, fac_high[...], fac_low[...])
        for b in range(2):
            rows_y = y[b * ROWS : (b + 1) * ROWS]
            y_buf[u, b] = rows_y
            flat = jnp.concatenate(
                [rows_y[:, g * LANES : (g + 1) * LANES] for g in range(GROUPS)], axis=0
            )
            for p in pieces:
                p.dense[1 + b] = flat[p.start : p.start + p.rows]
        for p in pieces:
            d = p.dense
            p.b3 = {}
            p.b3["up", 0] = remote(d.at[1], d.at[3], p.up)
            p.b3["down", 1] = remote(d.at[2], d.at[6], p.down)
            p.b3["up", 1] = remote(d.at[2], d.at[4], p.up)
            p.b3["down", 0] = remote(d.at[1], d.at[5], p.down)
        here = pl.ds(pl.multiple_of(core * HALF + u * ROWS, ROWS), ROWS)
        last_local.append(local(y_buf.at[u, core], owned.at[here, :]))
        give_owned.append(remote(y_buf.at[u, 1 - core], owned.at[here, :], sibling))

    def b3_far(pieces):
        for p in pieces:
            d = p.dense
            p.b3["up", 0].wait_recv()
            p.b3["far", 0] = remote(d.at[3], d.at[7], p.up)
            p.b3["down", 1].wait_recv()
            p.b3["far", 1] = remote(d.at[6], d.at[8], p.down)

    def b2_start(pieces):
        for p in pieces:
            d = p.dense
            for key in (("up", 1), ("down", 0), ("far", 0), ("far", 1)):
                p.b3[key].wait_recv()
            p.up, p.down = neighbour(p.order[1], 1), neighbour(p.order[1], 3)
            p.b2 = {}
            p.b2["up", 0] = remote(d.at[pl.ds(1, 4)], d.at[pl.ds(9, 4)], p.up)
            p.b2["down", 1] = remote(d.at[pl.ds(5, 4)], d.at[pl.ds(21, 4)], p.down)
            p.b2["up", 1] = remote(d.at[pl.ds(5, 4)], d.at[pl.ds(13, 4)], p.up)
            p.b2["down", 0] = remote(d.at[pl.ds(1, 4)], d.at[pl.ds(17, 4)], p.down)

    def b2_far(pieces):
        for p in pieces:
            d = p.dense
            p.b2["up", 0].wait_recv()
            p.b2["far", 0] = remote(d.at[pl.ds(9, 4)], d.at[pl.ds(25, 4)], p.up)
            p.b2["down", 1].wait_recv()
            p.b2["far", 1] = remote(d.at[pl.ds(21, 4)], d.at[pl.ds(29, 4)], p.down)

    def answer(p, i):
        return p.dense[tab[p.number, 2, i]]

    def b1_far(pieces):
        for p in pieces:
            for key in (("up", 1), ("down", 0), ("far", 0), ("far", 1)):
                p.b2[key].wait_recv()
            p.up, p.down = neighbour(p.order[0], 1), neighbour(p.order[0], 3)

            def body(h, p=p):
                for s in range(3):
                    p.b1_far_up[h * 3 + s] = answer(p, 48 + h * 8 + s)
                    p.b1_far_down[h * 3 + s] = answer(p, 51 + h * 8 + s)

            loop(2, body)
            p.b1_far = (
                remote(p.b1_far_up, p.b1_got_far_up, p.up),
                remote(p.b1_far_down, p.b1_got_far_down, p.down),
            )

    def b1_near(pieces):
        for p in pieces:

            def body(h, p=p):
                for s in range(3):
                    p.b1_up[6 + h * 3 + s] = answer(p, 35 + h * 8 + s)
                    p.b1_down[h * 3 + s] = answer(p, 16 + h * 8 + s)

            loop(2, body)
            p.b1_near = [
                remote(p.b1_up.at[pl.ds(6, 6)], p.b1_got_up.at[pl.ds(6, 6)], p.up),
                remote(p.b1_down.at[pl.ds(0, 6)], p.b1_got_down.at[pl.ds(0, 6)], p.down),
            ]

    def b1_merge(pieces):
        for p in pieces:
            p.b1_far[0].wait_recv()

            def up_body(h, p=p):
                for s in range(3):
                    p.b1_up[h * 3 + s] = p.b1_got_far_up[h * 3 + s] + answer(p, 32 + h * 8 + s)

            loop(2, up_body)
            p.b1_near.append(remote(p.b1_up.at[pl.ds(0, 6)], p.b1_got_up.at[pl.ds(0, 6)], p.up))
            p.b1_far[1].wait_recv()

            def down_body(h, p=p):
                for s in range(3):
                    p.b1_down[6 + h * 3 + s] = p.b1_got_far_down[h * 3 + s] + answer(p, 19 + h * 8 + s)

            loop(2, down_body)
            p.b1_near.append(
                remote(p.b1_down.at[pl.ds(6, 6)], p.b1_got_down.at[pl.ds(6, 6)], p.down)
            )

    last_remote = []

    def finish(pieces):
        u = pieces[0].stream
        for p in pieces:
            for copy in p.b1_near:
                copy.wait_recv()

            def body(h, p=p):
                for t in range(2):
                    for s in range(3):
                        q = t * 6 + h * 3 + s
                        value = answer(p, h * 8 + t * 3 + s) + (p.b1_got_up[q] + p.b1_got_down[q])
                        done = 0
                        while done < p.rows:
                            g, r = divmod(p.start + done, ROWS)
                            n = min(ROWS - r, p.rows - done)
                            out_buf[u, h * 6 + t * 3 + s, pl.ds(r, n), pl.ds(g * LANES, LANES)] = value[
                                done : done + n
                            ]
                            done += n

            loop(2, body)
        here = pl.ds(pl.multiple_of(core * HALF + u * ROWS, ROWS), ROWS)
        last_remote.append(
            remote(out_buf.at[u, pl.ds(6, 6)], returned.at[:, here, :], sibling)
        )
        last_local.append(local(out_buf.at[u, pl.ds(0, 6)], returned.at[:, here, :]))

    get_factor.wait()
    high, low = split(fac[...])
    fac_high[...] = high
    fac_low[...] = low
    add_near_lists(first_stream)
    a2_far(first_stream)
    a2_near(first_stream)
    for name, chunks in (("up", FAR_UP[2:]), ("down", FAR_DOWN)):
        for chunk in chunks:
            send_far(second_stream, name, *chunk)
    add_near_lists(second_stream)
    a2_far(second_stream)
    a2_merge(first_stream)
    a2_near(second_stream)
    a2_merge(second_stream)
    a3_start(first_stream)
    a3_merge(first_stream)
    a3_start(second_stream)
    a3_end(first_stream)
    a3_merge(second_stream)
    update(first_stream)
    a3_end(second_stream)
    update(second_stream)
    b3_far(first_stream)
    b2_start(first_stream)
    b3_far(second_stream)
    b2_far(first_stream)
    b2_start(second_stream)
    b2_far(second_stream)
    b1_far(first_stream)
    b1_near(first_stream)
    b1_far(second_stream)
    b1_merge(first_stream)
    b1_near(second_stream)
    b1_merge(second_stream)
    finish(first_stream)
    finish(second_stream)
    for copy in last_local:
        copy.wait()
    for copy in give_owned + last_remote:
        copy.wait_recv()
    for copy in sent:
        copy.wait_send()


def local_step(blocks, features, col_ids, row_ids, factor):
    scratch = []
    for u in range(STREAMS):
        for _, rows in PIECES[u]:
            for _, depth in PIECE_BUFFERS:
                scratch.append(pltpu.VMEM((depth, rows, LANES), F32))
    scratch += [
        pltpu.VMEM((RING, B, BPR * B), F32),
        pltpu.VMEM((FT, B, FEAT), F32),
        pltpu.VMEM((FT * B, FEAT), BF16),
        pltpu.VMEM((FT * B, FEAT), BF16),
        pltpu.VMEM((BPR + 1, B, B), F32),
        pltpu.VMEM((2 * B, FT * B), BF16),
        pltpu.VMEM((2 * B, FT * B), BF16),
        pltpu.VMEM((SLOTS, 2, STREAMS, TILE_ROWS, LANES), F32),
        pltpu.VMEM((48, STREAMS, TILE_ROWS, LANES), F32),
        pltpu.VMEM((SLOTS, BPR), I32),
        pltpu.VMEM((16, LANES), I32),
        pltpu.SMEM((16, LANES), I32),
        pltpu.SMEM((SLOTS,), I32),
        pltpu.VMEM((8, LANES), I32),
        pltpu.VMEM((10, 16, LANES), I32),
        pltpu.VMEM((3, 8, LANES), I32),
        pltpu.SMEM((3, 8, LANES), I32),
        pltpu.VMEM((STREAMS, 2, TILE_ROWS, LANES), F32),
        pltpu.VMEM((STREAMS, 2, ROWS, FEAT), F32),
        pltpu.VMEM((STREAMS, 2 * SLOTS, ROWS, FEAT), F32),
        pltpu.VMEM((FEAT, FEAT), F32),
        pltpu.VMEM((FEAT, FEAT), BF16),
        pltpu.VMEM((FEAT, FEAT), BF16),
        pltpu.SemaphoreType.DMA((N_REMOTE,)),
        pltpu.SemaphoreType.DMA((N_REMOTE,)),
        pltpu.SemaphoreType.DMA((N_LOCAL,)),
    ]
    hbm = pl.BlockSpec(memory_space=pl.ANY)
    owned, returned = pl.pallas_call(
        kernel,
        in_specs=[hbm] * 5,
        out_specs=[hbm] * 2,
        out_shape=[
            jax.ShapeDtypeStruct((B, FEAT), F32),
            jax.ShapeDtypeStruct((SLOTS, B, FEAT), F32),
        ],
        scratch_shapes=scratch,
        compiler_params=pltpu.CompilerParams(
            collective_id=0, has_side_effects=True, vmem_limit_bytes=67043328
        ),
    )(blocks, features, col_ids, row_ids, factor)
    return owned, returned.reshape(SLOTS * B, FEAT)


def solution(mesh):
    return jax.shard_map(
        local_step,
        mesh=mesh,
        in_specs=(
            P(("gx", "gy"), None, None),
            P(("gx", "gy"), None, None),
            P(("gx", "gy"), None),
            P(("gx", "gy")),
            P(),
        ),
        out_specs=(P(("gx", "gy"), None), P(("gx", "gy"), None)),
        check_vma=False,
    )
```

time: 898 us -> 105 us (0.12); the launches traced: 887 us -> 105 us
  waiting for transfers between devices: 599 us -> 0 us
  matrix products: 109 us -> 0 us
  Pallas kernels: 0 us -> 100 us
  local copies, waits for them, and re-layouts: 100 us -> 4.34 us
  other arithmetic: 46.9 us -> 0 us
  starting transfers between devices: 30.9 us -> 0 us
    ppermute x17 -> x0, waiting for transfers between devices: 599 us -> none  [partner(): return lax.ppermute(value, axis, pairs)]
    dot_general x9 -> x0, matrix products: 109 us -> none  [the longest x6 92.9 us: local(): jnp.dot(blocks[slot_num], stacked, precision=HIGHEST, preferred_element_t...]
    pallas_call x0 -> x1, Pallas kernels: none -> 100 us  [local_step(): pl.pallas_call(kernel, in_specs=[hbm] * 5, out_specs=[hbm] * 2, out_shape...]
    gather x6 -> x0, local copies, waits for them, and re-layouts: 39.2 us -> none  [local(): features[col_ids[slot_num]].reshape(per_row * tile_rows, feat_width)]
    unnamed x34 -> x2, local copies, waits for them, and re-layouts: 36.1 us -> 4.34 us
    ppermute x17 -> x0, starting transfers between devices: 30.9 us -> none  [partner(): return lax.ppermute(value, axis, pairs)]
    select_n x20 -> x0, other arithmetic: 29.4 us -> none  [the longest x3 15.3 us: local(): jnp.where(kept_mask[:, None, None], values, 0.0)]
    slice x5 -> x0, local copies, waits for them, and re-layouts: 23.4 us -> none  [the longest x4 16.8 us: local(): incoming = partner(answers[count_kept:], ('gx', 'gy'), record[3])]
  transfers between devices with their start and end apart: 17 -> 0, of which waited for: 14 -> 0; matrix products, arithmetic and copies ran while one was open for 2% -> 0% of each run, Pallas kernels for 0% -> 0%
where the time goes in v2:
time: 105 us
  Pallas kernels  100 us (95%)
  local copies, waits for them, and re-layouts  4.34 us (4%)
    pallas_call x1, Pallas kernels, local_step(): pl.pallas_call(kernel, in_specs=[hbm] * 5, out_specs=[hbm] * 2, out_shape...  100 us
    unnamed x2, local copies, waits for them, and re-layouts  4.34 us

profile of v2, /device:TPU:1, one launch (start us, length us, event | category | flops | bytes accessed | tf_op | source)
XLA Modules:
  0.0 105.2 jit_solution(18206093576157021896)
XLA Ops:
  0.6 100.2 %shard_map.68 = (f32[128,512]{1,0:T(8,128)}, f32[6,128,512]{2,1,0:T(8,128)}) custom-call(f32[6,128,4096]{2,1,0:T(8,128)} %blocks.1, f32[16,128,512]{2,1,0:T(8,128)} %features.1, s32[6,32]{1,0:T(8,128)} %col_ids.1, s32[6]{0:T(128)} %row_ids.1, f32[512,512]{1,0:T(8,128)} %factor.1), custom_call_target="tpu_custom_call" | custom-call | tf_op jit(solution)/shard_map/pallas_call | solution.py:692
  100.9 1.7 %copy.9 = f32[128,512]{1,0:T(8,128)} copy(f32[128,512]{1,0:T(8,128)} %get-tuple-element.8) | data formatting | bytes 524288
  102.5 2.7 %copy.10 = f32[768,512]{1,0:T(8,128)} copy(f32[768,512]{1,0:T(8,128)} %bitcast.1) | data formatting | bytes 3145728

commit v3 on v2

v3 whole, which is shorter than its diff:
```python
import functools

import jax
import jax.numpy as jnp
from jax import lax
from jax.experimental import pallas as pl
from jax.experimental.pallas import tpu as pltpu
from jax.sharding import PartitionSpec as P

MESH = pl.DeviceIdType.MESH
F32 = jnp.float32
BF16 = jnp.bfloat16
I32 = jnp.int32

B = 128
FEAT = 512
SLOTS = 6
BPR = 32
FT = 16
HALF = B // 2
STREAMS = 2
ROWS = HALF // STREAMS
LANES = 128
GROUPS = FEAT // LANES
TILE_ROWS = ROWS * GROUPS
SHIFT = {"z": 5, "y": 3, "x": 1}
ORDERS = ("zyx", "yxz", "xzy")
PIECES = (((0, 48), (48, 40), (88, 40)), ((0, 40), (40, 48), (88, 40)))
CHUNKS = ((0, 1), (1, 1), (2, 2), (4, 2))
FAR_UP = ((0, 0), (1, 0), (0, 1), (1, 1), (0, 3))
FAR_DOWN = ((0, 2), (1, 2), (1, 3))


def split(value):
    high = value.astype(BF16)
    return high, (value - high.astype(F32)).astype(BF16)


def product(left_high, left_low, right_high, right_low):
    dot = functools.partial(jnp.dot, preferred_element_type=F32)
    return dot(left_high, right_high) + (dot(left_high, right_low) + dot(left_low, right_high))


PIECE_BUFFERS = (
    ("sums", 49),
    ("a2_far_up", 4),
    ("a2_far_down", 4),
    ("a2_got_far_up", 4),
    ("a2_got_far_down", 4),
    ("a2_up", 8),
    ("a2_down", 8),
    ("a2_got", 16),
    ("quarter", 8),
    ("a3_got_far", 2),
    ("a3_up", 1),
    ("a3_down", 1),
    ("a3_got", 4),
    ("dense", 33),
    ("b1_got_far_up", 6),
    ("b1_got_far_down", 6),
    ("b1_got", 24),
)
PIECE_SLOTS = 36 + 24 + 6 + 6 + 24 + 36
N_SEND = 32
N_RECV = 176
N_LOCAL = 20
RING = 4
VMEM_LIMIT = 62 << 20


class Piece:
    pass


def kernel(blocks, features, col_ids, row_ids, factor, out, *scratch):
    scratch = list(scratch)
    streams = []
    for u in range(STREAMS):
        pieces = []
        for number, (start, rows) in enumerate(PIECES[u]):
            piece = Piece()
            piece.number, piece.start, piece.rows, piece.order = number, start, rows, ORDERS[number]
            piece.stream = u
            for name, _ in PIECE_BUFFERS:
                setattr(piece, name, scratch.pop(0))
            piece.b1_far_up, piece.b1_far_down = piece.sums.at[pl.ds(1, 6)], piece.sums.at[pl.ds(7, 6)]
            piece.b1_up, piece.b1_down = piece.sums.at[pl.ds(13, 12)], piece.sums.at[pl.ds(25, 12)]
            piece.slots_sent = 0
            pieces.append(piece)
        streams.append(pieces)
    (
        blk, feat, f_high, f_low, chain, a_high, a_low, part, entries, cols, col_v, col_tab, ids,
        tile, lab, tab_v, tab, x_buf, y_buf, out_buf, fac, fac_high, fac_low,
        send_sem, recv_sem, local_sem,
    ) = scratch

    z = lax.axis_index("gx")
    gy = lax.axis_index("gy")
    core = gy % 2
    at = {"z": z, "y": gy // 8, "x": (gy // 2) % 4}

    def neighbour(axis, step):
        to = dict(at)
        to[axis] = (at[axis] + step) % 4
        return (to["z"], to["y"] * 8 + to["x"] * 2 + core)

    sibling = (z, gy - core + (1 - core))
    counts = {"send": 0, "recv": 0, "local": 0}
    sent = []

    def take(kind, limit):
        n = counts[kind]
        counts[kind] += 1
        assert n < limit
        return n

    def arrival():
        return recv_sem.at[take("recv", N_RECV)]

    for pieces in streams:
        for p in pieces:
            p.send = send_sem.at[take("send", N_SEND)]

    def remote(source, target, device, piece=None, recv=None):
        copy = pltpu.make_async_remote_copy(
            src_ref=source,
            dst_ref=target,
            send_sem=send_sem.at[take("send", N_SEND)] if piece is None else piece.send,
            recv_sem=arrival() if recv is None else recv,
            device_id=device,
            device_id_type=MESH,
        )
        copy.start()
        if piece is None:
            sent.append(copy)
        else:
            piece.slots_sent += source.shape[0] if len(source.shape) == 3 else 1
        return copy

    def wait_all(ref, sem):
        pltpu.make_async_copy(ref, ref, sem).wait()

    def local(source, target):
        copy = pltpu.make_async_copy(source, target, local_sem.at[take("local", N_LOCAL)])
        copy.start()
        return copy

    barrier = pltpu.get_barrier_semaphore()
    greeted = [sibling] + [neighbour(axis, step) for axis in "zyx" for step in (1, 3)]
    for device in greeted:
        pl.semaphore_signal(barrier, inc=1, device_id=device, device_id_type=MESH)
    get_cols = local(col_ids, cols)
    get_ids = local(row_ids, ids)
    get_feat = [local(features.at[pl.ds(0, 8)], feat.at[pl.ds(0, 8)])]
    get_blk = {0: local(blocks.at[0], blk.at[0])}
    get_feat.append(local(features.at[pl.ds(8, 8)], feat.at[pl.ds(8, 8)]))
    for k in range(1, RING):
        get_blk[k] = local(blocks.at[k], blk.at[k])
    get_factor = local(factor, fac)

    get_cols.wait()
    row = lax.broadcasted_iota(I32, (BPR, BPR), 0)
    lane = lax.broadcasted_iota(I32, (BPR, BPR), 1)
    for k in range(SLOTS):
        across = jnp.broadcast_to(cols[pl.ds(k, 1), :], (BPR, BPR))
        down = jnp.sum(jnp.where(row == lane, across, 0), axis=1, keepdims=True)
        col_v[pl.ds(2 * k, 1), pl.ds(0, BPR)] = jnp.max(
            jnp.where(jnp.logical_and(down == across, row < lane), row + 1, 0), axis=0, keepdims=True
        )
        col_v[pl.ds(2 * k + 1, 1), pl.ds(0, BPR)] = jnp.max(
            jnp.where(down == lane, row + 1, 0), axis=0, keepdims=True
        )
    get_ids.wait()
    line = lax.broadcasted_iota(I32, (8, LANES), 0)
    names = jnp.full((8, LANES), -1, I32)
    for s in range(SLOTS):
        names = jnp.where(line == s, ids[s], names)
    tile[...] = names
    chain[0] = jnp.zeros((B, B), F32)
    for pieces in streams:
        for p in pieces:
            p.sums[0] = jnp.zeros((p.rows, LANES), F32)
            p.dense[0] = jnp.zeros((p.rows, LANES), F32)

    get_col_tab = local(col_v, col_tab)

    def convert(first):
        def body(t, carry):
            high, low = split(feat[t])
            f_high[pl.ds(pl.multiple_of(t * B, B), B), :] = high
            f_low[pl.ds(pl.multiple_of(t * B, B), B), :] = low
            return carry

        lax.fori_loop(first, first + 8, body, 0)

    def gather_sums(k):
        get_blk[k].wait()
        held = blk.at[k % RING]

        for j in range(BPR):
            chain[j + 1] = held[:, pl.ds(j * B, B)] + chain[col_tab[2 * k, j]]
        for t in range(FT):
            high, low = split(chain[col_tab[2 * k + 1, t]])
            a_high[:, pl.ds(t * B, B)] = high
            a_low[:, pl.ds(t * B, B)] = low
        if k + RING < SLOTS:
            get_blk[k + RING] = local(blocks.at[k + RING], blk.at[k % RING])

    def make(k):
        gather_sums(k)
        result = product(a_high[...], a_low[...], f_high[...], f_low[...])
        for half in range(2):
            for u in range(STREAMS):
                first = half * HALF + u * ROWS
                for g in range(GROUPS):
                    part[k, half, u, pl.ds(g * ROWS, ROWS), :] = result[
                        first : first + ROWS, g * LANES : (g + 1) * LANES
                    ]

    give_part = {}

    def place_of(half, chunk):
        return half * SLOTS + CHUNKS[chunk][0]

    def send_part(chunk):
        first, number = CHUNKS[chunk]
        give_part[chunk] = remote(
            part.at[pl.ds(first, number), 1 - core],
            entries.at[pl.ds(place_of(1, chunk), number)],
            sibling,
        )

    WAYS = {"up": (1, 1), "down": (2, 3)}

    def send_list(pieces, half, chunk):
        first, number = CHUNKS[chunk]
        for p in pieces:
            here = pl.ds(p.start, p.rows)
            if half == 0:
                source = part.at[pl.ds(first, number), core, p.stream, here]
            else:
                source = entries.at[pl.ds(place_of(1, chunk), number), p.stream, here]
            for name, far in (("up", FAR_UP), ("down", FAR_DOWN)):
                order, to = WAYS[name]
                target = entries.at[pl.ds(order * 12 + place_of(half, chunk), number), p.stream, here]
                recv = None if (half, chunk) in far else p.list_recv
                p.lists[name, half, chunk] = remote(source, target, neighbour(p.order[0], to), p, recv)

    def send_far(pieces, half, chunk):
        name = "up" if (half, chunk) in FAR_UP else "down"
        order, to = WAYS[name]
        number = CHUNKS[chunk][1]
        for p in pieces:
            here = pl.ds(p.start, p.rows)
            p.lists[name, half, chunk].wait_recv()
            remote(
                entries.at[pl.ds(order * 12 + place_of(half, chunk), number), p.stream, here],
                entries.at[pl.ds(36 + place_of(half, chunk), number), p.stream, here],
                neighbour(p.order[0], to),
                p,
                p.far_recv,
            )

    for pieces in streams:
        for p in pieces:
            p.lists = {}
            p.list_recv, p.far_recv = arrival(), arrival()
    one, two = streams

    get_feat[0].wait()
    convert(0)
    get_feat[1].wait()
    convert(8)
    get_col_tab.wait()
    make(0)
    pl.semaphore_wait(barrier, len(greeted))
    give_names = remote(tile, lab.at[0, pl.ds(8, 8)], sibling)
    keep_names = local(tile, lab.at[0, pl.ds(0, 8)])
    send_part(0)
    send_list(one, 0, 0)
    send_list(two, 0, 0)
    make(1)
    send_part(1)
    give_part[0].wait_recv()
    send_list(one, 1, 0)
    send_list(two, 1, 0)
    send_list(one, 0, 1)
    send_list(two, 0, 1)
    keep_names.wait()
    give_names.wait_recv()
    lab_up, lab_down, lab_far = {}, {}, {}
    for j in range(3):
        lab_up[j] = remote(lab.at[0], lab.at[1 + 3 * j], neighbour(ORDERS[j][0], 1))
        lab_down[j] = remote(lab.at[0], lab.at[2 + 3 * j], neighbour(ORDERS[j][0], 3))
    make(2)
    give_part[1].wait_recv()
    send_list(one, 1, 1)
    send_list(two, 1, 1)
    make(3)
    send_part(2)
    send_list(one, 0, 2)
    send_far(one, 0, 0)
    send_far(one, 1, 0)
    make(4)
    give_part[2].wait_recv()
    send_list(one, 1, 2)
    for j in range(3):
        lab_up[j].wait_recv()
        lab_far[j] = remote(lab.at[1 + 3 * j], lab.at[3 + 3 * j], neighbour(ORDERS[j][0], 1))
    make(5)
    send_part(3)
    send_list(one, 0, 3)
    send_far(one, 0, 1)
    send_far(one, 1, 1)
    send_far(one, 0, 2)
    give_part[3].wait_recv()
    send_list(one, 1, 3)
    send_far(one, 1, 2)
    send_list(two, 0, 2)
    send_list(two, 1, 2)
    for chunk in FAR_UP[:4]:
        send_far(two, *chunk)

    def make_table(j):
        lab_down[j].wait_recv()
        lab_far[j].wait_recv()
        first, second, third = ORDERS[j]
        seen = jnp.concatenate([lab[0], lab[1 + 3 * j], lab[2 + 3 * j], lab[3 + 3 * j]], axis=0)
        row = lax.broadcasted_iota(I32, (64, LANES), 0)
        lane = lax.broadcasted_iota(I32, (64, LANES), 1)
        place_of_row = (row >> 4) * 12 + ((row >> 3) & 1) * 6 + (row & 7) + 1
        wanted = jnp.sum(jnp.where(row == lane, seen, 0), axis=0, keepdims=True)
        previous = jnp.max(
            jnp.where(jnp.logical_and(seen == wanted, row < lane), place_of_row, 0),
            axis=0,
            keepdims=True,
        )

        def step_of(order):
            return jnp.where(order == 1, 3, jnp.where(order == 2, 1, jnp.where(order == 3, 2, 0)))

        def order_of(step):
            return jnp.where(step == 0, 0, jnp.where(step == 3, 1, step + 1))

        named = (
            (at[first] << SHIFT[first])
            + (((at[second] + step_of((lane >> 3) & 3)) & 3) << SHIFT[second])
            + (((at[third] + step_of((lane >> 1) & 3)) & 3) << SHIFT[third])
            + (lane & 1)
        )
        last = jnp.max(jnp.where(seen == named, place_of_row, 0), axis=0, keepdims=True)
        place = (
            1
            + order_of((((wanted >> SHIFT[second]) & 3) - at[second]) & 3) * 8
            + order_of((((wanted >> SHIFT[third]) & 3) - at[third]) & 3) * 2
            + (wanted & 1)
        )
        place = jnp.where(((wanted >> SHIFT[first]) & 3) == at[first], place, 0)
        tab_v[j] = jnp.where(line == 0, previous, jnp.where(line == 1, last, place))

    for j in range(3):
        make_table(j)
    send_far(one, 0, 3)
    send_far(one, 1, 3)
    get_tab = local(tab_v, tab)
    send_list(two, 0, 3)
    send_list(two, 1, 3)
    get_tab.wait()

    def add_lists(pieces, order):
        for p in pieces:
            here = pl.ds(p.start, p.rows)
            for h in range(2):
                for s in range(SLOTS):
                    place = order * 12 + h * 6 + s
                    if order == 0 and h == 0:
                        value = part[s, core, p.stream, here]
                    else:
                        value = entries[place, p.stream, here]
                    p.sums[place + 1] = value + p.sums[tab[p.number, 0, order * 16 + h * 8 + s]]

    def add_near_lists(pieces):
        add_lists(pieces, 0)
        for p in pieces:
            wait_all(p.sums.at[pl.ds(0, 12)], p.list_recv)
        add_lists(pieces, 1)
        add_lists(pieces, 2)

    def pick(p, r):
        return p.sums[tab[p.number, 1, r]]

    def loop(n, body):
        def step(m, carry):
            body(m)
            return carry

        lax.fori_loop(0, n, step, 0)

    def a2_far(pieces):
        for p in pieces:
            wait_all(p.sums.at[pl.ds(0, 12)], p.far_recv)
            add_lists([p], 3)
            p.up, p.down = neighbour(p.order[1], 1), neighbour(p.order[1], 3)

            def body(m, p=p):
                p.a2_far_up[m] = pick(p, 24 + m)
                p.a2_far_down[m] = pick(p, 28 + m)

            loop(4, body)
            p.a2_far = (
                remote(p.a2_far_up, p.a2_got_far_up, p.up, p),
                remote(p.a2_far_down, p.a2_got_far_down, p.down, p),
            )
            p.a2_recv = arrival()

    def a2_near(pieces):
        for p in pieces:

            def body(m, p=p):
                p.a2_up[m + 4] = pick(p, 20 + m)
                p.a2_down[m] = pick(p, 8 + m)

            loop(4, body)
            remote(p.a2_up.at[pl.ds(4, 4)], p.a2_got.at[pl.ds(4, 4)], p.up, p, p.a2_recv)
            remote(p.a2_down.at[pl.ds(0, 4)], p.a2_got.at[pl.ds(8, 4)], p.down, p, p.a2_recv)

    def a2_merge(pieces):
        for p in pieces:
            p.a2_far[0].wait_recv()

            def up_body(m, p=p):
                p.a2_up[m] = p.a2_got_far_up[m] + pick(p, 16 + m)

            loop(4, up_body)
            remote(p.a2_up.at[pl.ds(0, 4)], p.a2_got.at[pl.ds(0, 4)], p.up, p, p.a2_recv)
            p.a2_far[1].wait_recv()

            def down_body(m, p=p):
                p.a2_down[m + 4] = p.a2_got_far_down[m] + pick(p, 12 + m)

            loop(4, down_body)
            remote(p.a2_down.at[pl.ds(4, 4)], p.a2_got.at[pl.ds(12, 4)], p.down, p, p.a2_recv)

    def a3_start(pieces):
        for p in pieces:
            wait_all(p.a2_got, p.a2_recv)

            def body(m, p=p):
                p.quarter[m] = pick(p, m) + (p.a2_got[m] + p.a2_got[8 + m])

            loop(8, body)
            p.up, p.down = neighbour(p.order[2], 1), neighbour(p.order[2], 3)
            p.a3_far = (
                remote(p.quarter.at[6], p.a3_got_far.at[0], p.up, p),
                remote(p.quarter.at[7], p.a3_got_far.at[1], p.down, p),
            )
            p.a3_recv = arrival()
            remote(p.quarter.at[5], p.a3_got.at[1], p.up, p, p.a3_recv)
            remote(p.quarter.at[2], p.a3_got.at[2], p.down, p, p.a3_recv)

    def a3_merge(pieces):
        for p in pieces:
            p.a3_far[0].wait_recv()
            p.a3_up[0] = p.quarter[4] + p.a3_got_far[0]
            p.a3_far[1].wait_recv()
            p.a3_down[0] = p.quarter[3] + p.a3_got_far[1]
            remote(p.a3_up.at[0], p.a3_got.at[0], p.up, p, p.a3_recv)
            remote(p.a3_down.at[0], p.a3_got.at[3], p.down, p, p.a3_recv)

    def a3_end(pieces):
        for p in pieces:
            wait_all(p.a3_got, p.a3_recv)
            for b in range(2):
                x_buf[p.stream, b, pl.ds(p.start, p.rows), :] = jnp.tanh(
                    p.quarter[b] + (p.a3_got[b] + p.a3_got[2 + b])
                )

    last = []

    def update(pieces):
        u = pieces[0].stream
        x = jnp.concatenate(
            [
                jnp.concatenate(
                    [x_buf[u, b, pl.ds(g * ROWS, ROWS), :] for g in range(GROUPS)], axis=1
                )
                for b in range(2)
            ],
            axis=0,
        )
        x_high, x_low = split(x)
        y = product(x_high, x_low, fac_high[...], fac_low[...])
        for b in range(2):
            rows_y = y[b * ROWS : (b + 1) * ROWS]
            flat = jnp.concatenate(
                [rows_y[:, g * LANES : (g + 1) * LANES] for g in range(GROUPS)], axis=0
            )
            for p in pieces:
                p.dense[1 + b] = flat[p.start : p.start + p.rows]
        for p in pieces:
            d = p.dense
            p.b3_recv = arrival()
            p.b3_up = remote(d.at[1], d.at[3], p.up, p)
            p.b3_down = remote(d.at[2], d.at[6], p.down, p)
            remote(d.at[2], d.at[4], p.up, p, p.b3_recv)
            remote(d.at[1], d.at[5], p.down, p, p.b3_recv)
        here = pl.ds(pl.multiple_of(core * HALF + u * ROWS, ROWS), ROWS)
        mine = jnp.where(core == 0, y[:ROWS], y[ROWS:])
        y_buf[u] = jnp.where(core == 0, y[ROWS:], y[:ROWS])
        out[0, here, :] = mine
        last.append(remote(y_buf.at[u], out.at[0, here, :], sibling))

    def b3_far(pieces):
        for p in pieces:
            d = p.dense
            p.b3_up.wait_recv()
            remote(d.at[3], d.at[7], p.up, p, p.b3_recv)
            p.b3_down.wait_recv()
            remote(d.at[6], d.at[8], p.down, p, p.b3_recv)

    def b2_start(pieces):
        for p in pieces:
            d = p.dense
            wait_all(d.at[pl.ds(5, 4)], p.b3_recv)
            p.up, p.down = neighbour(p.order[1], 1), neighbour(p.order[1], 3)
            p.b2_recv = arrival()
            p.b2_up = remote(d.at[pl.ds(1, 4)], d.at[pl.ds(9, 4)], p.up, p)
            p.b2_down = remote(d.at[pl.ds(5, 4)], d.at[pl.ds(21, 4)], p.down, p)
            remote(d.at[pl.ds(5, 4)], d.at[pl.ds(13, 4)], p.up, p, p.b2_recv)
            remote(d.at[pl.ds(1, 4)], d.at[pl.ds(17, 4)], p.down, p, p.b2_recv)

    def b2_far(pieces):
        for p in pieces:
            d = p.dense
            p.b2_up.wait_recv()
            remote(d.at[pl.ds(9, 4)], d.at[pl.ds(25, 4)], p.up, p, p.b2_recv)
            p.b2_down.wait_recv()
            remote(d.at[pl.ds(21, 4)], d.at[pl.ds(29, 4)], p.down, p, p.b2_recv)

    def answer(p, i):
        return p.dense[tab[p.number, 2, i]]

    def b1_far(pieces):
        for p in pieces:
            wait_all(p.dense.at[pl.ds(17, 16)], p.b2_recv)
            p.up, p.down = neighbour(p.order[0], 1), neighbour(p.order[0], 3)

            def body(h, p=p):
                for s in range(3):
                    p.b1_far_up[h * 3 + s] = answer(p, 48 + h * 8 + s)
                    p.b1_far_down[h * 3 + s] = answer(p, 51 + h * 8 + s)

            loop(2, body)
            p.b1_far = (
                remote(p.b1_far_up, p.b1_got_far_up, p.up, p),
                remote(p.b1_far_down, p.b1_got_far_down, p.down, p),
            )
            p.b1_recv = arrival()

    def b1_near(pieces):
        for p in pieces:

            def body(h, p=p):
                for s in range(3):
                    p.b1_up[6 + h * 3 + s] = answer(p, 35 + h * 8 + s)
                    p.b1_down[h * 3 + s] = answer(p, 16 + h * 8 + s)

            loop(2, body)
            remote(p.b1_up.at[pl.ds(6, 6)], p.b1_got.at[pl.ds(6, 6)], p.up, p, p.b1_recv)
            remote(p.b1_down.at[pl.ds(0, 6)], p.b1_got.at[pl.ds(12, 6)], p.down, p, p.b1_recv)

    def b1_merge(pieces):
        for p in pieces:
            p.b1_far[0].wait_recv()

            def up_body(h, p=p):
                for s in range(3):
                    p.b1_up[h * 3 + s] = p.b1_got_far_up[h * 3 + s] + answer(p, 32 + h * 8 + s)

            loop(2, up_body)
            remote(p.b1_up.at[pl.ds(0, 6)], p.b1_got.at[pl.ds(0, 6)], p.up, p, p.b1_recv)
            p.b1_far[1].wait_recv()

            def down_body(h, p=p):
                for s in range(3):
                    p.b1_down[6 + h * 3 + s] = p.b1_got_far_down[h * 3 + s] + answer(p, 19 + h * 8 + s)

            loop(2, down_body)
            remote(p.b1_down.at[pl.ds(6, 6)], p.b1_got.at[pl.ds(18, 6)], p.down, p, p.b1_recv)

    def finish(pieces):
        u = pieces[0].stream
        first = core * HALF + u * ROWS
        for p in pieces:
            wait_all(p.b1_got, p.b1_recv)

            def body(n, p=p):
                t, s = n // 3, n % 3
                for h in (1, 0):
                    q = t * 6 + h * 3 + s
                    value = answer(p, h * 8 + n) + (p.b1_got[q] + p.b1_got[12 + q])
                    done = 0
                    while done < p.rows:
                        g, r = divmod(p.start + done, ROWS)
                        size = min(ROWS - r, p.rows - done)
                        across = pl.ds(g * LANES, LANES)
                        if h == 0:
                            rows = pl.ds(pl.multiple_of(first + r, 8), size)
                            out[1 + n, rows, across] = value[done : done + size]
                        else:
                            out_buf[u, n, pl.ds(r, size), across] = value[done : done + size]
                        done += size

            loop(SLOTS, body)
        here = pl.ds(pl.multiple_of(first, ROWS), ROWS)
        last.append(remote(out_buf.at[u], out.at[pl.ds(1, SLOTS), here, :], sibling))

    get_factor.wait()
    high, low = split(fac[...])
    fac_high[...] = high
    fac_low[...] = low
    add_near_lists(one)
    send_far(two, 0, 2)
    send_far(two, 1, 2)
    a2_far(one)
    a2_near(one)
    send_far(two, 0, 3)
    send_far(two, 1, 3)
    add_near_lists(two)
    a2_merge(one)
    a2_far(two)
    a3_start(one)
    a2_near(two)
    a2_merge(two)
    a3_merge(one)
    a3_end(one)
    update(one)
    a3_start(two)
    b3_far(one)
    a3_merge(two)
    b2_start(one)
    a3_end(two)
    update(two)
    b2_far(one)
    b3_far(two)
    b2_start(two)
    b1_far(one)
    b2_far(two)
    b1_near(one)
    b1_merge(one)
    b1_far(two)
    b1_near(two)
    finish(one)
    b1_merge(two)
    finish(two)
    for copy in last:
        copy.wait_recv()
    for copy in sent:
        copy.wait_send()
    for pieces in streams:
        for p in pieces:
            assert p.slots_sent == PIECE_SLOTS
            wait_all(blocks.at[:, pl.ds(0, 88), pl.ds(0, 32 * p.rows)], p.send)


def output_kernel(held, owned, returned, sems):
    copies = (
        pltpu.make_async_copy(held.at[0], owned, sems.at[0]),
        pltpu.make_async_copy(held.at[pl.ds(1, SLOTS)], returned, sems.at[1]),
    )
    for copy in copies:
        copy.start()
    for copy in copies:
        copy.wait()


def local_step(blocks, features, col_ids, row_ids, factor):
    scratch = []
    for u in range(STREAMS):
        for _, rows in PIECES[u]:
            for _, depth in PIECE_BUFFERS:
                scratch.append(pltpu.VMEM((depth, rows, LANES), F32))
    scratch += [
        pltpu.VMEM((RING, B, BPR * B), F32),
        pltpu.VMEM((FT, B, FEAT), F32),
        pltpu.VMEM((FT * B, FEAT), BF16),
        pltpu.VMEM((FT * B, FEAT), BF16),
        pltpu.VMEM((BPR + 1, B, B), F32),
        pltpu.VMEM((B, FT * B), BF16),
        pltpu.VMEM((B, FT * B), BF16),
        pltpu.VMEM((SLOTS, 2, STREAMS, TILE_ROWS, LANES), F32),
        pltpu.VMEM((48, STREAMS, TILE_ROWS, LANES), F32),
        pltpu.VMEM((SLOTS, BPR), I32),
        pltpu.VMEM((16, LANES), I32),
        pltpu.SMEM((16, LANES), I32),
        pltpu.SMEM((SLOTS,), I32),
        pltpu.VMEM((8, LANES), I32),
        pltpu.VMEM((10, 16, LANES), I32),
        pltpu.VMEM((3, 8, LANES), I32),
        pltpu.SMEM((3, 8, LANES), I32),
        pltpu.VMEM((STREAMS, 2, TILE_ROWS, LANES), F32),
        pltpu.VMEM((STREAMS, ROWS, FEAT), F32),
        pltpu.VMEM((STREAMS, SLOTS, ROWS, FEAT), F32),
        pltpu.VMEM((FEAT, FEAT), F32),
        pltpu.VMEM((FEAT, FEAT), BF16),
        pltpu.VMEM((FEAT, FEAT), BF16),
        pltpu.SemaphoreType.DMA((N_SEND,)),
        pltpu.SemaphoreType.DMA((N_RECV,)),
        pltpu.SemaphoreType.DMA((N_LOCAL,)),
    ]
    hbm = pl.BlockSpec(memory_space=pl.ANY)
    held = pl.pallas_call(
        kernel,
        in_specs=[hbm] * 5,
        out_specs=pl.BlockSpec(memory_space=pltpu.VMEM),
        out_shape=jax.ShapeDtypeStruct((1 + SLOTS, B, FEAT), F32),
        scratch_shapes=scratch,
        compiler_params=pltpu.CompilerParams(
            collective_id=0, has_side_effects=True, vmem_limit_bytes=VMEM_LIMIT
        ),
    )(blocks, features, col_ids, row_ids, factor)
    owned, returned = pl.pallas_call(
        output_kernel,
        in_specs=[pl.BlockSpec(memory_space=pltpu.VMEM)],
        out_specs=[hbm] * 2,
        out_shape=[
            jax.ShapeDtypeStruct((B, FEAT), F32),
            jax.ShapeDtypeStruct((SLOTS, B, FEAT), F32),
        ],
        scratch_shapes=[pltpu.SemaphoreType.DMA((2,))],
        compiler_params=pltpu.CompilerParams(vmem_limit_bytes=1 << 20),
    )(held)
    return owned, returned.reshape(SLOTS * B, FEAT)


def solution(mesh):
    return jax.shard_map(
        local_step,
        mesh=mesh,
        in_specs=(
            P(("gx", "gy"), None, None),
            P(("gx", "gy"), None, None),
            P(("gx", "gy"), None),
            P(("gx", "gy")),
            P(),
        ),
        out_specs=(P(("gx", "gy"), None), P(("gx", "gy"), None)),
        check_vma=False,
    )
```

time: 105 us -> 97.4 us (0.928)
  Pallas kernels: 100 us -> 95.1 us
  local copies, waits for them, and re-layouts: 4.34 us -> 1.49 us
    pallas_call x1 -> x2, Pallas kernels: 100 us -> 95.1 us  [the longest x1 93.8 us: local_step(): pl.pallas_call(kernel, in_specs=[hbm] * 5, out_specs=pl.BlockSpec(memory_...]
    unnamed x2, local copies, waits for them, and re-layouts: 4.34 us -> 1.49 us
where the time goes in v3:
time: 97.4 us; the launch traced here: 97.2 us
  Pallas kernels  95.1 us (98%)
  local copies, waits for them, and re-layouts  1.49 us (2%)
    pallas_call x1, Pallas kernels, local_step(): pl.pallas_call(kernel, in_specs=[hbm] * 5, out_specs=pl.BlockSpec(memory_...  93.8 us

profile of v3, /device:TPU:1, one launch (start us, length us, event | category | flops | bytes accessed | tf_op | source)
XLA Modules:
  0.0 97.2 jit_solution(12805992311407856685)
XLA Ops:
  0.6 93.8 %shard_map.68.held = f32[7,128,512]{2,1,0:T(8,128)} custom-call(f32[6,128,4096]{2,1,0:T(8,128)} %blocks.1, f32[16,128,512]{2,1,0:T(8,128)} %features.1, s32[6,32]{1,0:T(8,128)} %col_ids.1, s32[6]{0:T(128)} %row_ids.1, f32[512,512]{1,0:T(8,128)} %factor.1), custom_call_target="tpu_custom_call" | custom-call | tf_op jit(solution)/shard_map/pallas_call | solution.py:712
  94.5 0.0 copy-start
  94.5 1.5 %copy-done = f32[7,128,512]{2,1,0:T(8,128)S(1)} copy-done((f32[7,128,512]{2,1,0:T(8,128)S(1)}, f32[7,128,512]{2,1,0:T(8,128)}, u32[]{:S(2)}) %copy-start) | copy-done | bytes 1835032
  96.0 1.2 %shard_map.69 = (f32[128,512]{1,0:T(8,128)}, f32[6,128,512]{2,1,0:T(8,128)}) custom-call(f32[7,128,512]{2,1,0:T(8,128)S(1)} %copy-done), custom_call_target="tpu_custom_call" | custom-call | tf_op jit(solution)/shard_map/pallas_call | solution.py:722
Async XLA Ops:
  94.5 1.5 %copy-start = (f32[7,128,512]{2,1,0:T(8,128)S(1)}, f32[7,128,512]{2,1,0:T(8,128)}, u32[]{:S(2)}) copy-start(f32[7,128,512]{2,1,0:T(8,128)} %shard_map.68.held) | copy-start | bytes 5505028

commit v4 on v3

v4 whole, which is shorter than its diff:
```python
import functools

import jax
import jax.numpy as jnp
from jax import lax
from jax.experimental import pallas as pl
from jax.experimental.pallas import tpu as pltpu
from jax.sharding import PartitionSpec as P

MESH = pl.DeviceIdType.MESH
F32 = jnp.float32
BF16 = jnp.bfloat16
I32 = jnp.int32

B = 128
FEAT = 512
SLOTS = 6
BPR = 32
FT = 16
HALF = B // 2
STREAMS = 4
ROWS = HALF // STREAMS
LANES = 128
GROUPS = FEAT // LANES
TILE_ROWS = ROWS * GROUPS
SHIFT = {"z": 5, "y": 3, "x": 1}
ORDERS = ("zyx", "yxz", "xzy")
PIECES = (
    ((0, 24), (24, 24), (48, 16)),
    ((0, 24), (24, 16), (40, 24)),
    ((0, 16), (16, 24), (40, 24)),
    ((0, 24), (24, 24), (48, 16)),
)
CHUNKS = ((0, 1), (1, 1), (2, 2), (4, 2))
FAR_UP = ((0, 0), (1, 0), (0, 1), (1, 1), (0, 3))
FAR_DOWN = ((0, 2), (1, 2), (1, 3))


def split(value):
    high = value.astype(BF16)
    return high, (value - high.astype(F32)).astype(BF16)


def product(left_high, left_low, right_high, right_low):
    dot = functools.partial(jnp.dot, preferred_element_type=F32)
    return dot(left_high, right_high) + (dot(left_high, right_low) + dot(left_low, right_high))


PIECE_BUFFERS = (
    ("sums", 49),
    ("a2_far_up", 4),
    ("a2_far_down", 4),
    ("a2_got_far_up", 4),
    ("a2_got_far_down", 4),
    ("a2_up", 8),
    ("a2_down", 8),
    ("a2_got", 16),
    ("quarter", 8),
    ("a3_got_far", 2),
    ("a3_up", 1),
    ("a3_down", 1),
    ("a3_got", 4),
    ("dense", 33),
    ("b1_got_far_up", 6),
    ("b1_got_far_down", 6),
    ("b1_got", 24),
)
STREAM_SLOTS = 36 + 24 + 6 + 6 + 24 + 36
N_SEND = 32
N_RECV = 110
N_LOCAL = 14
RING = 4
VMEM_LIMIT = 58 << 20

(
    MAKE, GIVE, SEND, PASS_ON, TABLES, NEAR, A2_FAR, A2_NEAR, A2_MERGE, A3,
    A3_MERGE, UPDATE, B3_FAR, B2, B2_FAR, B1_FAR, B1_NEAR, B1_MERGE, FINISH,
) = range(19)
ORDER = (
    (MAKE, 0), (GIVE, 0), (SEND, 0, 0, 0), (SEND, 2, 0, 0), (SEND, 1, 0, 0), (SEND, 3, 0, 0),
    (MAKE, 1), (GIVE, 1), (SEND, 0, 0, 1), (SEND, 2, 1, 0), (SEND, 3, 1, 0), (MAKE, 2),
    (SEND, 0, 1, 1), (SEND, 2, 1, 1), (MAKE, 3), (GIVE, 2), (SEND, 2, 0, 2), (SEND, 0, 0, 2),
    (SEND, 1, 0, 2), (MAKE, 4), (SEND, 3, 1, 2), (SEND, 1, 1, 2), (SEND, 2, 1, 2), (MAKE, 5),
    (GIVE, 3), (SEND, 1, 0, 1), (SEND, 1, 1, 1), (PASS_ON, 0, 1, 1), (SEND, 1, 1, 0),
    (SEND, 0, 1, 0), (SEND, 3, 0, 1), (SEND, 0, 1, 2), (SEND, 0, 0, 3), (SEND, 1, 0, 3),
    (PASS_ON, 3, 0, 0), (PASS_ON, 0, 0, 1), (PASS_ON, 2, 0, 0), (PASS_ON, 2, 1, 0),
    (PASS_ON, 3, 1, 0), (TABLES,), (SEND, 0, 1, 3), (PASS_ON, 1, 1, 2), (PASS_ON, 2, 0, 2),
    (PASS_ON, 3, 1, 2), (SEND, 1, 1, 3), (PASS_ON, 0, 0, 2), (PASS_ON, 0, 0, 0), (PASS_ON, 2, 1, 1),
    (PASS_ON, 1, 0, 2), (PASS_ON, 1, 0, 0), (PASS_ON, 2, 1, 2), (PASS_ON, 1, 0, 1),
    (PASS_ON, 1, 1, 1), (PASS_ON, 1, 1, 0), (PASS_ON, 0, 1, 0), (PASS_ON, 3, 0, 1),
    (PASS_ON, 0, 1, 2), (PASS_ON, 0, 0, 3), (PASS_ON, 1, 0, 3), (PASS_ON, 0, 1, 3), (SEND, 2, 1, 3),
    (SEND, 3, 0, 2), (SEND, 2, 0, 1), (NEAR, 0), (SEND, 2, 0, 3), (PASS_ON, 1, 1, 3), (NEAR, 1),
    (SEND, 3, 0, 3), (SEND, 3, 1, 3), (SEND, 3, 1, 1), (A2_FAR, 0), (PASS_ON, 2, 1, 3),
    (A2_NEAR, 0), (PASS_ON, 3, 0, 2), (PASS_ON, 2, 0, 1), (PASS_ON, 2, 0, 3), (NEAR, 2),
    (A2_FAR, 1), (PASS_ON, 3, 0, 3), (PASS_ON, 3, 1, 3), (PASS_ON, 3, 1, 1), (NEAR, 3),
    (A2_MERGE, 0), (A2_NEAR, 1), (A2_FAR, 2), (A2_NEAR, 2), (A2_MERGE, 1), (A3, 0), (A2_FAR, 3),
    (A2_MERGE, 2), (A2_NEAR, 3), (A3, 1), (A3_MERGE, 0), (A2_MERGE, 3), (A3, 2), (A3_MERGE, 1),
    (UPDATE, 0), (A3, 3), (A3_MERGE, 2), (UPDATE, 1), (B3_FAR, 0), (A3_MERGE, 3), (UPDATE, 2),
    (B3_FAR, 1), (B2, 0), (UPDATE, 3), (B3_FAR, 2), (B2, 1), (B2_FAR, 0), (B3_FAR, 3), (B2, 2),
    (B2_FAR, 1), (B1_FAR, 0), (B2, 3), (B2_FAR, 2), (B1_FAR, 1), (B1_NEAR, 1), (B2_FAR, 3),
    (B1_NEAR, 0), (B1_MERGE, 0), (B1_MERGE, 1), (B1_FAR, 3), (B1_FAR, 2), (B1_NEAR, 2), (FINISH, 0),
    (FINISH, 1), (B1_NEAR, 3), (B1_MERGE, 3), (B1_MERGE, 2), (FINISH, 3), (FINISH, 2),
)


class Piece:
    pass


class Stream:
    pass


def kernel(blocks, features, col_ids, row_ids, factor, out, *scratch):
    scratch = list(scratch)
    streams = []
    for u in range(STREAMS):
        stream = Stream()
        stream.number, stream.pieces, stream.elements_sent = u, [], 0
        for number, (start, rows) in enumerate(PIECES[u]):
            p = Piece()
            p.number, p.start, p.rows = number, start, rows
            for name, _ in PIECE_BUFFERS:
                setattr(p, name, scratch.pop(0))
            p.b1_far_up, p.b1_far_down = p.sums.at[pl.ds(1, 6)], p.sums.at[pl.ds(7, 6)]
            p.b1_up, p.b1_down = p.sums.at[pl.ds(13, 12)], p.sums.at[pl.ds(25, 12)]
            stream.pieces.append(p)
        streams.append(stream)
    (
        blk, feat, f_high, f_low, chain, a_high, a_low, part, entries, cols, col_v, col_tab, ids,
        tile, lab, tab_v, tab, x_buf, y_buf, out_buf, fac, fac_high, fac_low,
        send_sem, recv_sem, local_sem,
    ) = scratch

    z = lax.axis_index("gx")
    gy = lax.axis_index("gy")
    core = gy % 2
    at = {"z": z, "y": gy // 8, "x": (gy // 2) % 4}

    def neighbour(axis, step):
        to = dict(at)
        to[axis] = (at[axis] + step) % 4
        return (to["z"], to["y"] * 8 + to["x"] * 2 + core)

    sibling = (z, gy - core + (1 - core))
    counts = {"send": 0, "recv": 0, "local": 0}
    sent = []

    def take(kind, limit):
        n = counts[kind]
        counts[kind] += 1
        assert n < limit
        return n

    def arrival():
        return recv_sem.at[take("recv", N_RECV)]

    for stream in streams:
        stream.send = send_sem.at[take("send", N_SEND)]
        for p in stream.pieces:
            p.stream = stream
            p.ways = [(neighbour(axis, 1), neighbour(axis, 3)) for axis in ORDERS[p.number]]

    def remote(source, target, device, stream=None, recv=None):
        copy = pltpu.make_async_remote_copy(
            src_ref=source,
            dst_ref=target,
            send_sem=send_sem.at[take("send", N_SEND)] if stream is None else stream.send,
            recv_sem=arrival() if recv is None else recv,
            device_id=device,
            device_id_type=MESH,
        )
        copy.start()
        if stream is None:
            sent.append(copy)
        else:
            elements = 1
            for size in source.shape:
                elements *= size
            stream.elements_sent += elements
        return copy

    def wait_slots(stream, slots, sem):
        ref = entries.at[pl.ds(0, slots), stream.number]
        pltpu.make_async_copy(ref, ref, sem).wait()

    def local(source, target):
        copy = pltpu.make_async_copy(source, target, local_sem.at[take("local", N_LOCAL)])
        copy.start()
        return copy

    barrier = pltpu.get_barrier_semaphore()
    greeted = [sibling] + [neighbour(axis, step) for axis in "zyx" for step in (1, 3)]
    for device in greeted:
        pl.semaphore_signal(barrier, inc=1, device_id=device, device_id_type=MESH)
    get_cols = local(col_ids, cols)
    get_ids = local(row_ids, ids)
    get_feat = [local(features.at[pl.ds(0, 8)], feat.at[pl.ds(0, 8)])]
    get_blk = {0: local(blocks.at[0], blk.at[0])}
    get_feat.append(local(features.at[pl.ds(8, 8)], feat.at[pl.ds(8, 8)]))
    for k in range(1, RING):
        get_blk[k] = local(blocks.at[k], blk.at[k])
    get_factor = local(factor, fac)

    get_cols.wait()
    row = lax.broadcasted_iota(I32, (BPR, BPR), 0)
    lane = lax.broadcasted_iota(I32, (BPR, BPR), 1)
    for k in range(SLOTS):
        across = jnp.broadcast_to(cols[pl.ds(k, 1), :], (BPR, BPR))
        down = jnp.sum(jnp.where(row == lane, across, 0), axis=1, keepdims=True)
        col_v[pl.ds(2 * k, 1), pl.ds(0, BPR)] = jnp.max(
            jnp.where(jnp.logical_and(down == across, row < lane), row + 1, 0), axis=0, keepdims=True
        )
        col_v[pl.ds(2 * k + 1, 1), pl.ds(0, BPR)] = jnp.max(
            jnp.where(down == lane, row + 1, 0), axis=0, keepdims=True
        )
    get_ids.wait()
    line = lax.broadcasted_iota(I32, (8, LANES), 0)
    names = jnp.full((8, LANES), -1, I32)
    for s in range(SLOTS):
        names = jnp.where(line == s, ids[s], names)
    tile[...] = names
    chain[0] = jnp.zeros((B, B), F32)
    for stream in streams:
        for p in stream.pieces:
            p.sums[0] = jnp.zeros((p.rows, LANES), F32)
            p.dense[0] = jnp.zeros((p.rows, LANES), F32)

    get_col_tab = local(col_v, col_tab)

    def convert(first):
        def body(t, carry):
            high, low = split(feat[t])
            f_high[pl.ds(pl.multiple_of(t * B, B), B), :] = high
            f_low[pl.ds(pl.multiple_of(t * B, B), B), :] = low
            return carry

        lax.fori_loop(first, first + 8, body, 0)

    def gather_sums(k):
        get_blk[k].wait()
        held = blk.at[k % RING]

        for j in range(BPR):
            chain[j + 1] = held[:, pl.ds(j * B, B)] + chain[col_tab[2 * k, j]]
        for t in range(FT):
            high, low = split(chain[col_tab[2 * k + 1, t]])
            a_high[:, pl.ds(t * B, B)] = high
            a_low[:, pl.ds(t * B, B)] = low
        if k + RING < SLOTS:
            get_blk[k + RING] = local(blocks.at[k + RING], blk.at[k % RING])

    def make(k):
        gather_sums(k)
        result = product(a_high[...], a_low[...], f_high[...], f_low[...])
        for half in range(2):
            for u in range(STREAMS):
                first = half * HALF + u * ROWS
                for g in range(GROUPS):
                    part[k, half, u, pl.ds(g * ROWS, ROWS), :] = result[
                        first : first + ROWS, g * LANES : (g + 1) * LANES
                    ]

    give_part = {}

    def place_of(half, chunk):
        return half * SLOTS + CHUNKS[chunk][0]

    def send_part(chunk):
        first, number = CHUNKS[chunk]
        give_part[chunk] = remote(
            part.at[pl.ds(first, number), 1 - core],
            entries.at[pl.ds(place_of(1, chunk), number)],
            sibling,
        )

    WAYS = {"up": 1, "down": 2}

    def send_list(stream, half, chunk):
        first, number = CHUNKS[chunk]
        if half == 1 and chunk not in arrived:
            arrived.add(chunk)
            give_part[chunk].wait_recv()
        stream.lists[half, chunk] = arrival()
        for p in stream.pieces:
            here = pl.ds(p.start, p.rows)
            if half == 0:
                source = part.at[pl.ds(first, number), core, stream.number, here]
            else:
                source = entries.at[pl.ds(place_of(1, chunk), number), stream.number, here]
            for name, far, device in zip(("up", "down"), (FAR_UP, FAR_DOWN), p.ways[0]):
                target = entries.at[
                    pl.ds(WAYS[name] * 12 + place_of(half, chunk), number), stream.number, here
                ]
                recv = stream.lists[half, chunk] if (half, chunk) in far else stream.list_recv
                remote(source, target, device, stream, recv)

    def send_far(stream, half, chunk):
        up = (half, chunk) in FAR_UP
        number = CHUNKS[chunk][1]
        wait_slots(stream, number, stream.lists[half, chunk])
        for p in stream.pieces:
            here = pl.ds(p.start, p.rows)
            remote(
                entries.at[
                    pl.ds(WAYS["up" if up else "down"] * 12 + place_of(half, chunk), number),
                    stream.number,
                    here,
                ],
                entries.at[pl.ds(36 + place_of(half, chunk), number), stream.number, here],
                p.ways[0][0 if up else 1],
                stream,
                stream.far_recv,
            )

    arrived = set()
    for stream in streams:
        stream.lists = {}
        stream.list_recv, stream.far_recv = arrival(), arrival()

    def make_table(j):
        lab_down[j].wait_recv()
        lab_far[j].wait_recv()
        first, second, third = ORDERS[j]
        seen = jnp.concatenate([lab[0], lab[1 + 3 * j], lab[2 + 3 * j], lab[3 + 3 * j]], axis=0)
        row = lax.broadcasted_iota(I32, (64, LANES), 0)
        lane = lax.broadcasted_iota(I32, (64, LANES), 1)
        place_of_row = (row >> 4) * 12 + ((row >> 3) & 1) * 6 + (row & 7) + 1
        wanted = jnp.sum(jnp.where(row == lane, seen, 0), axis=0, keepdims=True)
        previous = jnp.max(
            jnp.where(jnp.logical_and(seen == wanted, row < lane), place_of_row, 0),
            axis=0,
            keepdims=True,
        )

        def step_of(order):
            return jnp.where(order == 1, 3, jnp.where(order == 2, 1, jnp.where(order == 3, 2, 0)))

        def order_of(step):
            return jnp.where(step == 0, 0, jnp.where(step == 3, 1, step + 1))

        named = (
            (at[first] << SHIFT[first])
            + (((at[second] + step_of((lane >> 3) & 3)) & 3) << SHIFT[second])
            + (((at[third] + step_of((lane >> 1) & 3)) & 3) << SHIFT[third])
            + (lane & 1)
        )
        last = jnp.max(jnp.where(seen == named, place_of_row, 0), axis=0, keepdims=True)
        place = (
            1
            + order_of((((wanted >> SHIFT[second]) & 3) - at[second]) & 3) * 8
            + order_of((((wanted >> SHIFT[third]) & 3) - at[third]) & 3) * 2
            + (wanted & 1)
        )
        place = jnp.where(((wanted >> SHIFT[first]) & 3) == at[first], place, 0)
        tab_v[j] = jnp.where(line == 0, previous, jnp.where(line == 1, last, place))

    def add_list(stream, order):
        for h in range(2):
            for slot in range(SLOTS):
                place = order * 12 + h * 6 + slot
                for p in stream.pieces:
                    here = pl.ds(p.start, p.rows)
                    if order == 0 and h == 0:
                        value = part[slot, core, stream.number, here]
                    else:
                        value = entries[place, stream.number, here]
                    p.sums[place + 1] = value + p.sums[tab[p.number, 0, order * 16 + h * 8 + slot]]

    def near_lists(stream):
        add_list(stream, 0)
        wait_slots(stream, 12, stream.list_recv)
        add_list(stream, 1)
        add_list(stream, 2)

    def pick(p, r):
        return p.sums[tab[p.number, 1, r]]

    def loop(stream, n, body):
        def step(m, carry):
            for p in stream.pieces:
                body(p, m)
            return carry

        lax.fori_loop(0, n, step, 0)

    def a2_far(stream):
        wait_slots(stream, 12, stream.far_recv)
        add_list(stream, 3)

        def body(p, m):
            p.a2_far_up[m] = pick(p, 24 + m)
            p.a2_far_down[m] = pick(p, 28 + m)

        loop(stream, 4, body)
        stream.a2_far, stream.a2_recv = arrival(), arrival()
        for p in stream.pieces:
            up, down = p.ways[1]
            remote(p.a2_far_up, p.a2_got_far_up, up, stream, stream.a2_far)
            remote(p.a2_far_down, p.a2_got_far_down, down, stream, stream.a2_far)

    def a2_near(stream):
        def body(p, m):
            p.a2_up[m + 4] = pick(p, 20 + m)
            p.a2_down[m] = pick(p, 8 + m)

        loop(stream, 4, body)
        for p in stream.pieces:
            up, down = p.ways[1]
            remote(p.a2_up.at[pl.ds(4, 4)], p.a2_got.at[pl.ds(4, 4)], up, stream, stream.a2_recv)
            remote(p.a2_down.at[pl.ds(0, 4)], p.a2_got.at[pl.ds(8, 4)], down, stream, stream.a2_recv)

    def a2_merge(stream):
        wait_slots(stream, 8, stream.a2_far)

        def body(p, m):
            p.a2_up[m] = p.a2_got_far_up[m] + pick(p, 16 + m)
            p.a2_down[m + 4] = p.a2_got_far_down[m] + pick(p, 12 + m)

        loop(stream, 4, body)
        for p in stream.pieces:
            up, down = p.ways[1]
            remote(p.a2_up.at[pl.ds(0, 4)], p.a2_got.at[pl.ds(0, 4)], up, stream, stream.a2_recv)
            remote(p.a2_down.at[pl.ds(4, 4)], p.a2_got.at[pl.ds(12, 4)], down, stream, stream.a2_recv)

    def a3_start(stream):
        wait_slots(stream, 16, stream.a2_recv)

        def body(p, m):
            p.quarter[m] = pick(p, m) + (p.a2_got[m] + p.a2_got[8 + m])

        loop(stream, 8, body)
        stream.a3_far, stream.a3_recv = arrival(), arrival()
        for p in stream.pieces:
            up, down = p.ways[2]
            remote(p.quarter.at[6], p.a3_got_far.at[0], up, stream, stream.a3_far)
            remote(p.quarter.at[7], p.a3_got_far.at[1], down, stream, stream.a3_far)
        for p in stream.pieces:
            up, down = p.ways[2]
            remote(p.quarter.at[5], p.a3_got.at[1], up, stream, stream.a3_recv)
            remote(p.quarter.at[2], p.a3_got.at[2], down, stream, stream.a3_recv)

    def a3_merge(stream):
        wait_slots(stream, 2, stream.a3_far)
        for p in stream.pieces:
            p.a3_up[0] = p.quarter[4] + p.a3_got_far[0]
            p.a3_down[0] = p.quarter[3] + p.a3_got_far[1]
        for p in stream.pieces:
            up, down = p.ways[2]
            remote(p.a3_up.at[0], p.a3_got.at[0], up, stream, stream.a3_recv)
            remote(p.a3_down.at[0], p.a3_got.at[3], down, stream, stream.a3_recv)

    last = []

    def update(stream):
        u = stream.number
        wait_slots(stream, 4, stream.a3_recv)
        for p in stream.pieces:
            for b in range(2):
                x_buf[u, b, pl.ds(p.start, p.rows), :] = jnp.tanh(
                    p.quarter[b] + (p.a3_got[b] + p.a3_got[2 + b])
                )
        x = jnp.concatenate(
            [
                jnp.concatenate(
                    [x_buf[u, b, pl.ds(g * ROWS, ROWS), :] for g in range(GROUPS)], axis=1
                )
                for b in range(2)
            ],
            axis=0,
        )
        x_high, x_low = split(x)
        y = product(x_high, x_low, fac_high[...], fac_low[...])
        for b in range(2):
            rows_y = y[b * ROWS : (b + 1) * ROWS]
            flat = jnp.concatenate(
                [rows_y[:, g * LANES : (g + 1) * LANES] for g in range(GROUPS)], axis=0
            )
            for p in stream.pieces:
                p.dense[1 + b] = flat[p.start : p.start + p.rows]
        stream.b3_far, stream.b3_recv = arrival(), arrival()
        for p in stream.pieces:
            d, (up, down) = p.dense, p.ways[2]
            remote(d.at[1], d.at[3], up, stream, stream.b3_far)
            remote(d.at[2], d.at[6], down, stream, stream.b3_far)
        for p in stream.pieces:
            d, (up, down) = p.dense, p.ways[2]
            remote(d.at[2], d.at[4], up, stream, stream.b3_recv)
            remote(d.at[1], d.at[5], down, stream, stream.b3_recv)
        here = pl.ds(pl.multiple_of(core * HALF + u * ROWS, ROWS), ROWS)
        out[0, here, :] = jnp.where(core == 0, y[:ROWS], y[ROWS:])
        y_buf[u] = jnp.where(core == 0, y[ROWS:], y[:ROWS])
        last.append(remote(y_buf.at[u], out.at[0, here, :], sibling))

    def b3_far(stream):
        wait_slots(stream, 2, stream.b3_far)
        for p in stream.pieces:
            d, (up, down) = p.dense, p.ways[2]
            remote(d.at[3], d.at[7], up, stream, stream.b3_recv)
            remote(d.at[6], d.at[8], down, stream, stream.b3_recv)

    def b2_start(stream):
        wait_slots(stream, 4, stream.b3_recv)
        stream.b2_far, stream.b2_recv = arrival(), arrival()
        for p in stream.pieces:
            d, (up, down) = p.dense, p.ways[1]
            remote(d.at[pl.ds(1, 4)], d.at[pl.ds(9, 4)], up, stream, stream.b2_far)
            remote(d.at[pl.ds(5, 4)], d.at[pl.ds(21, 4)], down, stream, stream.b2_far)
        for p in stream.pieces:
            d, (up, down) = p.dense, p.ways[1]
            remote(d.at[pl.ds(5, 4)], d.at[pl.ds(13, 4)], up, stream, stream.b2_recv)
            remote(d.at[pl.ds(1, 4)], d.at[pl.ds(17, 4)], down, stream, stream.b2_recv)

    def b2_far(stream):
        wait_slots(stream, 8, stream.b2_far)
        for p in stream.pieces:
            d, (up, down) = p.dense, p.ways[1]
            remote(d.at[pl.ds(9, 4)], d.at[pl.ds(25, 4)], up, stream, stream.b2_recv)
            remote(d.at[pl.ds(21, 4)], d.at[pl.ds(29, 4)], down, stream, stream.b2_recv)

    def answer(p, i):
        return p.dense[tab[p.number, 2, i]]

    def b1_far(stream):
        wait_slots(stream, 16, stream.b2_recv)

        def body(p, h):
            for s in range(3):
                p.b1_far_up[h * 3 + s] = answer(p, 48 + h * 8 + s)
                p.b1_far_down[h * 3 + s] = answer(p, 51 + h * 8 + s)

        loop(stream, 2, body)
        stream.b1_far, stream.b1_recv = arrival(), arrival()
        for p in stream.pieces:
            up, down = p.ways[0]
            remote(p.b1_far_up, p.b1_got_far_up, up, stream, stream.b1_far)
            remote(p.b1_far_down, p.b1_got_far_down, down, stream, stream.b1_far)

    def b1_near(stream):
        def body(p, h):
            for s in range(3):
                p.b1_up[6 + h * 3 + s] = answer(p, 35 + h * 8 + s)
                p.b1_down[h * 3 + s] = answer(p, 16 + h * 8 + s)

        loop(stream, 2, body)
        for p in stream.pieces:
            up, down = p.ways[0]
            remote(p.b1_up.at[pl.ds(6, 6)], p.b1_got.at[pl.ds(6, 6)], up, stream, stream.b1_recv)
            remote(p.b1_down.at[pl.ds(0, 6)], p.b1_got.at[pl.ds(12, 6)], down, stream, stream.b1_recv)

    def b1_merge(stream):
        wait_slots(stream, 12, stream.b1_far)

        def body(p, h):
            for s in range(3):
                p.b1_up[h * 3 + s] = p.b1_got_far_up[h * 3 + s] + answer(p, 32 + h * 8 + s)
                p.b1_down[6 + h * 3 + s] = p.b1_got_far_down[h * 3 + s] + answer(p, 19 + h * 8 + s)

        loop(stream, 2, body)
        for p in stream.pieces:
            up, down = p.ways[0]
            remote(p.b1_up.at[pl.ds(0, 6)], p.b1_got.at[pl.ds(0, 6)], up, stream, stream.b1_recv)
            remote(p.b1_down.at[pl.ds(6, 6)], p.b1_got.at[pl.ds(18, 6)], down, stream, stream.b1_recv)

    def finish(stream):
        u = stream.number
        first = core * HALF + u * ROWS
        wait_slots(stream, 24, stream.b1_recv)

        def body(p, n):
            t, s = n // 3, n % 3
            for h in (1, 0):
                q = t * 6 + h * 3 + s
                value = answer(p, h * 8 + n) + (p.b1_got[q] + p.b1_got[12 + q])
                done = 0
                while done < p.rows:
                    g, r = divmod(p.start + done, ROWS)
                    size = min(ROWS - r, p.rows - done)
                    across = pl.ds(g * LANES, LANES)
                    if h == 0:
                        rows = pl.ds(pl.multiple_of(first + r, 8), size)
                        out[1 + n, rows, across] = value[done : done + size]
                    else:
                        out_buf[u, n, pl.ds(r, size), across] = value[done : done + size]
                    done += size

        loop(stream, SLOTS, body)
        here = pl.ds(pl.multiple_of(first, ROWS), ROWS)
        last.append(remote(out_buf.at[u], out.at[pl.ds(1, SLOTS), here, :], sibling))

    get_feat[0].wait()
    convert(0)
    get_feat[1].wait()
    convert(8)
    get_col_tab.wait()
    lab_up, lab_down, lab_far = {}, {}, {}
    waiting = {}

    def product_block(k):
        make(k)
        if k == 0:
            pl.semaphore_wait(barrier, len(greeted))
            waiting["give"] = remote(tile, lab.at[0, pl.ds(8, 8)], sibling)
            waiting["keep"] = local(tile, lab.at[0, pl.ds(0, 8)])
        if k == 1:
            waiting["keep"].wait()
            waiting["give"].wait_recv()
            for j in range(3):
                lab_up[j] = remote(lab.at[0], lab.at[1 + 3 * j], neighbour(ORDERS[j][0], 1))
                lab_down[j] = remote(lab.at[0], lab.at[2 + 3 * j], neighbour(ORDERS[j][0], 3))
        if k == 4:
            for j in range(3):
                lab_up[j].wait_recv()
                lab_far[j] = remote(
                    lab.at[1 + 3 * j], lab.at[3 + 3 * j], neighbour(ORDERS[j][0], 1)
                )

    def tables():
        for j in range(3):
            make_table(j)
        get_factor.wait()
        high, low = split(fac[...])
        fac_high[...] = high
        fac_low[...] = low
        local(tab_v, tab).wait()

    blocks_of = {
        MAKE: product_block, GIVE: send_part, SEND: send_list, PASS_ON: send_far, TABLES: tables,
        NEAR: near_lists, A2_FAR: a2_far, A2_NEAR: a2_near, A2_MERGE: a2_merge, A3: a3_start,
        A3_MERGE: a3_merge, UPDATE: update, B3_FAR: b3_far, B2: b2_start, B2_FAR: b2_far,
        B1_FAR: b1_far, B1_NEAR: b1_near, B1_MERGE: b1_merge, FINISH: finish,
    }
    for kind, *numbers in ORDER:
        if kind in (MAKE, GIVE, TABLES):
            blocks_of[kind](*numbers)
        else:
            blocks_of[kind](streams[numbers[0]], *numbers[1:])
    for copy in last:
        copy.wait_recv()
    for copy in sent:
        copy.wait_send()
    for stream in streams:
        assert stream.elements_sent == STREAM_SLOTS * TILE_ROWS * LANES
        ref = blocks.at[:, pl.ds(0, 88), pl.ds(0, 32 * TILE_ROWS)]
        pltpu.make_async_copy(ref, ref, stream.send).wait()


def output_kernel(held, owned, returned, sems):
    copies = (
        pltpu.make_async_copy(held.at[0], owned, sems.at[0]),
        pltpu.make_async_copy(held.at[pl.ds(1, SLOTS)], returned, sems.at[1]),
    )
    for copy in copies:
        copy.start()
    for copy in copies:
        copy.wait()


def local_step(blocks, features, col_ids, row_ids, factor):
    scratch = []
    for u in range(STREAMS):
        for _, rows in PIECES[u]:
            for _, depth in PIECE_BUFFERS:
                scratch.append(pltpu.VMEM((depth, rows, LANES), F32))
    scratch += [
        pltpu.VMEM((RING, B, BPR * B), F32),
        pltpu.VMEM((FT, B, FEAT), F32),
        pltpu.VMEM((FT * B, FEAT), BF16),
        pltpu.VMEM((FT * B, FEAT), BF16),
        pltpu.VMEM((BPR + 1, B, B), F32),
        pltpu.VMEM((B, FT * B), BF16),
        pltpu.VMEM((B, FT * B), BF16),
        pltpu.VMEM((SLOTS, 2, STREAMS, TILE_ROWS, LANES), F32),
        pltpu.VMEM((48, STREAMS, TILE_ROWS, LANES), F32),
        pltpu.VMEM((SLOTS, BPR), I32),
        pltpu.VMEM((16, LANES), I32),
        pltpu.SMEM((16, LANES), I32),
        pltpu.SMEM((SLOTS,), I32),
        pltpu.VMEM((8, LANES), I32),
        pltpu.VMEM((10, 16, LANES), I32),
        pltpu.VMEM((3, 8, LANES), I32),
        pltpu.SMEM((3, 8, LANES), I32),
        pltpu.VMEM((STREAMS, 2, TILE_ROWS, LANES), F32),
        pltpu.VMEM((STREAMS, ROWS, FEAT), F32),
        pltpu.VMEM((STREAMS, SLOTS, ROWS, FEAT), F32),
        pltpu.VMEM((FEAT, FEAT), F32),
        pltpu.VMEM((FEAT, FEAT), BF16),
        pltpu.VMEM((FEAT, FEAT), BF16),
        pltpu.SemaphoreType.DMA((N_SEND,)),
        pltpu.SemaphoreType.DMA((N_RECV,)),
        pltpu.SemaphoreType.DMA((N_LOCAL,)),
    ]
    hbm = pl.BlockSpec(memory_space=pl.ANY)
    held = pl.pallas_call(
        kernel,
        in_specs=[hbm] * 5,
        out_specs=pl.BlockSpec(memory_space=pltpu.VMEM),
        out_shape=pltpu.VMEM((1 + SLOTS, B, FEAT), F32),
        scratch_shapes=scratch,
        compiler_params=pltpu.CompilerParams(
            collective_id=0, has_side_effects=True, vmem_limit_bytes=VMEM_LIMIT
        ),
    )(blocks, features, col_ids, row_ids, factor)
    owned, returned = pl.pallas_call(
        output_kernel,
        in_specs=[pl.BlockSpec(memory_space=pltpu.VMEM)],
        out_specs=[hbm] * 2,
        out_shape=[
            jax.ShapeDtypeStruct((B, FEAT), F32),
            jax.ShapeDtypeStruct((SLOTS, B, FEAT), F32),
        ],
        scratch_shapes=[pltpu.SemaphoreType.DMA((2,))],
        compiler_params=pltpu.CompilerParams(vmem_limit_bytes=1 << 20),
    )(held)
    return owned, returned.reshape(SLOTS * B, FEAT)


def solution(mesh):
    return jax.shard_map(
        local_step,
        mesh=mesh,
        in_specs=(
            P(("gx", "gy"), None, None),
            P(("gx", "gy"), None, None),
            P(("gx", "gy"), None),
            P(("gx", "gy")),
            P(),
        ),
        out_specs=(P(("gx", "gy"), None), P(("gx", "gy"), None)),
        check_vma=False,
    )
```

time: 97.4 us -> 88.3 us (0.907)
  Pallas kernels: 95.1 us -> 87.6 us
  local copies, waits for them, and re-layouts: 1.49 us -> 0 us
    pallas_call x1, Pallas kernels: 93.8 us -> 86.3 us  [local_step(): pl.pallas_call(kernel, in_specs=[hbm] * 5, out_specs=pl.BlockSpec(memory_...]
    unnamed x2 -> x0, local copies, waits for them, and re-layouts: 1.49 us -> none
where the time goes in v4:
time: 88.3 us; the launch traced here: 88.2 us
  Pallas kernels  87.6 us (99%)
    pallas_call x1, Pallas kernels, local_step(): pl.pallas_call(kernel, in_specs=[hbm] * 5, out_specs=pl.BlockSpec(memory_...  86.3 us

profile of v4, /device:TPU:1, one launch (start us, length us, event | category | flops | bytes accessed | tf_op | source)
XLA Modules:
  0.0 88.2 jit_solution(7076836625078834581)
XLA Ops:
  0.6 86.3 %shard_map.68.held = f32[7,128,512]{2,1,0:T(8,128)S(1)} custom-call(f32[6,128,4096]{2,1,0:T(8,128)} %blocks.1, f32[16,128,512]{2,1,0:T(8,128)} %features.1, s32[6,32]{1,0:T(8,128)} %col_ids.1, s32[6]{0:T(128)} %row_ids.1, f32[512,512]{1,0:T(8,128)} %factor.1), custom_call_target="tpu_custom_call" | custom-call | tf_op jit(solution)/shard_map/pallas_call | solution.py:694
  87.0 1.2 %shard_map.69 = (f32[128,512]{1,0:T(8,128)}, f32[6,128,512]{2,1,0:T(8,128)}) custom-call(f32[7,128,512]{2,1,0:T(8,128)S(1)} %shard_map.68.held), custom_call_target="tpu_custom_call" | custom-call | tf_op jit(solution)/shard_map/pallas_call | solution.py:704

commit v5 on v4

--- a/solution.py
+++ b/solution.py
@@ -66,9 +66,9 @@
     ("b1_got", 24),
 )
 STREAM_SLOTS = 36 + 24 + 6 + 6 + 24 + 36
-N_SEND = 32
+N_SEND = 36
 N_RECV = 110
-N_LOCAL = 14
+N_LOCAL = 16
 RING = 4
 VMEM_LIMIT = 58 << 20
 
@@ -77,30 +77,31 @@
     A3_MERGE, UPDATE, B3_FAR, B2, B2_FAR, B1_FAR, B1_NEAR, B1_MERGE, FINISH,
 ) = range(19)
 ORDER = (
-    (MAKE, 0), (GIVE, 0), (SEND, 0, 0, 0), (SEND, 2, 0, 0), (SEND, 1, 0, 0), (SEND, 3, 0, 0),
-    (MAKE, 1), (GIVE, 1), (SEND, 0, 0, 1), (SEND, 2, 1, 0), (SEND, 3, 1, 0), (MAKE, 2),
-    (SEND, 0, 1, 1), (SEND, 2, 1, 1), (MAKE, 3), (GIVE, 2), (SEND, 2, 0, 2), (SEND, 0, 0, 2),
-    (SEND, 1, 0, 2), (MAKE, 4), (SEND, 3, 1, 2), (SEND, 1, 1, 2), (SEND, 2, 1, 2), (MAKE, 5),
-    (GIVE, 3), (SEND, 1, 0, 1), (SEND, 1, 1, 1), (PASS_ON, 0, 1, 1), (SEND, 1, 1, 0),
-    (SEND, 0, 1, 0), (SEND, 3, 0, 1), (SEND, 0, 1, 2), (SEND, 0, 0, 3), (SEND, 1, 0, 3),
-    (PASS_ON, 3, 0, 0), (PASS_ON, 0, 0, 1), (PASS_ON, 2, 0, 0), (PASS_ON, 2, 1, 0),
-    (PASS_ON, 3, 1, 0), (TABLES,), (SEND, 0, 1, 3), (PASS_ON, 1, 1, 2), (PASS_ON, 2, 0, 2),
-    (PASS_ON, 3, 1, 2), (SEND, 1, 1, 3), (PASS_ON, 0, 0, 2), (PASS_ON, 0, 0, 0), (PASS_ON, 2, 1, 1),
-    (PASS_ON, 1, 0, 2), (PASS_ON, 1, 0, 0), (PASS_ON, 2, 1, 2), (PASS_ON, 1, 0, 1),
-    (PASS_ON, 1, 1, 1), (PASS_ON, 1, 1, 0), (PASS_ON, 0, 1, 0), (PASS_ON, 3, 0, 1),
-    (PASS_ON, 0, 1, 2), (PASS_ON, 0, 0, 3), (PASS_ON, 1, 0, 3), (PASS_ON, 0, 1, 3), (SEND, 2, 1, 3),
-    (SEND, 3, 0, 2), (SEND, 2, 0, 1), (NEAR, 0), (SEND, 2, 0, 3), (PASS_ON, 1, 1, 3), (NEAR, 1),
-    (SEND, 3, 0, 3), (SEND, 3, 1, 3), (SEND, 3, 1, 1), (A2_FAR, 0), (PASS_ON, 2, 1, 3),
-    (A2_NEAR, 0), (PASS_ON, 3, 0, 2), (PASS_ON, 2, 0, 1), (PASS_ON, 2, 0, 3), (NEAR, 2),
-    (A2_FAR, 1), (PASS_ON, 3, 0, 3), (PASS_ON, 3, 1, 3), (PASS_ON, 3, 1, 1), (NEAR, 3),
-    (A2_MERGE, 0), (A2_NEAR, 1), (A2_FAR, 2), (A2_NEAR, 2), (A2_MERGE, 1), (A3, 0), (A2_FAR, 3),
-    (A2_MERGE, 2), (A2_NEAR, 3), (A3, 1), (A3_MERGE, 0), (A2_MERGE, 3), (A3, 2), (A3_MERGE, 1),
-    (UPDATE, 0), (A3, 3), (A3_MERGE, 2), (UPDATE, 1), (B3_FAR, 0), (A3_MERGE, 3), (UPDATE, 2),
-    (B3_FAR, 1), (B2, 0), (UPDATE, 3), (B3_FAR, 2), (B2, 1), (B2_FAR, 0), (B3_FAR, 3), (B2, 2),
-    (B2_FAR, 1), (B1_FAR, 0), (B2, 3), (B2_FAR, 2), (B1_FAR, 1), (B1_NEAR, 1), (B2_FAR, 3),
-    (B1_NEAR, 0), (B1_MERGE, 0), (B1_MERGE, 1), (B1_FAR, 3), (B1_FAR, 2), (B1_NEAR, 2), (FINISH, 0),
-    (FINISH, 1), (B1_NEAR, 3), (B1_MERGE, 3), (B1_MERGE, 2), (FINISH, 3), (FINISH, 2),
+    (MAKE, 0), (GIVE, 0), (SEND, 0, 0, 0), (SEND, 1, 0, 0), (MAKE, 1), (GIVE, 1), (SEND, 2, 0, 0),
+    (SEND, 2, 1, 0), (SEND, 2, 0, 1), (SEND, 3, 0, 0), (SEND, 0, 1, 0), (SEND, 1, 1, 0),
+    (SEND, 3, 0, 1), (MAKE, 2), (SEND, 1, 0, 1), (SEND, 3, 1, 1), (SEND, 0, 1, 1), (SEND, 3, 1, 0),
+    (SEND, 0, 0, 1), (SEND, 1, 1, 1), (MAKE, 3), (GIVE, 2), (SEND, 2, 0, 2), (SEND, 1, 0, 2),
+    (SEND, 0, 0, 2), (SEND, 2, 1, 1), (SEND, 3, 0, 2), (MAKE, 4), (SEND, 3, 1, 2), (SEND, 2, 1, 2),
+    (MAKE, 5), (GIVE, 3), (SEND, 3, 0, 3), (PASS_ON, 3, 1, 1), (PASS_ON, 3, 0, 0), (SEND, 2, 0, 3),
+    (SEND, 3, 1, 3), (PASS_ON, 1, 0, 2), (PASS_ON, 2, 1, 0), (SEND, 1, 1, 2), (PASS_ON, 3, 0, 1),
+    (SEND, 1, 1, 3), (SEND, 2, 1, 3), (SEND, 0, 1, 3), (PASS_ON, 3, 1, 0), (TABLES,),
+    (PASS_ON, 2, 0, 0), (PASS_ON, 3, 0, 2), (PASS_ON, 3, 1, 2), (PASS_ON, 3, 0, 3),
+    (PASS_ON, 1, 1, 1), (PASS_ON, 1, 0, 1), (PASS_ON, 3, 1, 3), (PASS_ON, 1, 0, 0),
+    (PASS_ON, 2, 0, 2), (SEND, 1, 0, 3), (PASS_ON, 2, 1, 1), (PASS_ON, 2, 1, 2), (PASS_ON, 0, 0, 2),
+    (NEAR, 3), (PASS_ON, 0, 1, 0), (PASS_ON, 2, 0, 3), (PASS_ON, 2, 0, 1), (PASS_ON, 2, 1, 3),
+    (PASS_ON, 1, 1, 2), (SEND, 0, 0, 3), (PASS_ON, 1, 1, 0), (SEND, 0, 1, 2), (A2_FAR, 3),
+    (PASS_ON, 1, 1, 3), (PASS_ON, 1, 0, 3), (PASS_ON, 0, 1, 3), (PASS_ON, 0, 0, 0), (A2_NEAR, 3),
+    (NEAR, 2), (PASS_ON, 0, 1, 1), (A2_FAR, 2), (PASS_ON, 0, 1, 2), (PASS_ON, 0, 0, 1),
+    (PASS_ON, 0, 0, 3), (A2_MERGE, 3), (NEAR, 0), (NEAR, 1), (A2_FAR, 1), (A2_NEAR, 2),
+    (A2_MERGE, 2), (A2_FAR, 0), (A3, 3), (A2_NEAR, 1), (A2_MERGE, 1), (A3, 2), (A3_MERGE, 3),
+    (A2_NEAR, 0), (A2_MERGE, 0), (A3, 1), (A3_MERGE, 2), (UPDATE, 3), (A3, 0), (A3_MERGE, 1),
+    (UPDATE, 2), (B3_FAR, 3), (A3_MERGE, 0), (UPDATE, 1), (B3_FAR, 2), (B2, 3), (UPDATE, 0),
+    (B3_FAR, 1), (B2, 2), (B2_FAR, 3), (B3_FAR, 0), (B2, 1), (B2_FAR, 2), (B1_FAR, 3), (B1_NEAR, 3),
+    (B2_FAR, 1), (B2, 0), (B1_MERGE, 3), (B1_FAR, 2), (B2_FAR, 0), (B1_FAR, 1), (B1_NEAR, 1),
+    (B1_NEAR, 2), (B1_FAR, 0), (FINISH, 3), (B1_NEAR, 0), (B1_MERGE, 2), (B1_MERGE, 1),
+    (B1_MERGE, 0), (FINISH, 1), (FINISH, 2), (FINISH, 0),
 )
+PACED = (A2_FAR, A3, UPDATE, B2, B2_FAR, B1_FAR, B1_MERGE)
 
 
 class Piece:
@@ -129,7 +130,7 @@
     (
         blk, feat, f_high, f_low, chain, a_high, a_low, part, entries, cols, col_v, col_tab, ids,
         tile, lab, tab_v, tab, x_buf, y_buf, out_buf, fac, fac_high, fac_low,
-        send_sem, recv_sem, local_sem,
+        send_sem, recv_sem, local_sem, pace_sem,
     ) = scratch
 
     z = lax.axis_index("gx")
@@ -190,14 +191,15 @@
         return copy
 
     barrier = pltpu.get_barrier_semaphore()
-    greeted = [sibling] + [neighbour(axis, step) for axis in "zyx" for step in (1, 3)]
+    greeted = [sibling] + [neighbour(axis, step) for axis in "zyx" for step in (1, 2, 3)]
     for device in greeted:
         pl.semaphore_signal(barrier, inc=1, device_id=device, device_id_type=MESH)
     get_cols = local(col_ids, cols)
     get_ids = local(row_ids, ids)
-    get_feat = [local(features.at[pl.ds(0, 8)], feat.at[pl.ds(0, 8)])]
     get_blk = {0: local(blocks.at[0], blk.at[0])}
-    get_feat.append(local(features.at[pl.ds(8, 8)], feat.at[pl.ds(8, 8)]))
+    get_feat = [
+        local(features.at[pl.ds(4 * i, 4)], feat.at[pl.ds(4 * i, 4)]) for i in range(FT // 4)
+    ]
     for k in range(1, RING):
         get_blk[k] = local(blocks.at[k], blk.at[k])
     get_factor = local(factor, fac)
@@ -225,7 +227,6 @@
         for p in stream.pieces:
             p.sums[0] = jnp.zeros((p.rows, LANES), F32)
             p.dense[0] = jnp.zeros((p.rows, LANES), F32)
-
     get_col_tab = local(col_v, col_tab)
 
     def convert(first):
@@ -235,7 +236,7 @@
             f_low[pl.ds(pl.multiple_of(t * B, B), B), :] = low
             return carry
 
-        lax.fori_loop(first, first + 8, body, 0)
+        lax.fori_loop(first, first + 4, body, 0)
 
     def gather_sums(k):
         get_blk[k].wait()
@@ -250,8 +251,29 @@
         if k + RING < SLOTS:
             get_blk[k + RING] = local(blocks.at[k + RING], blk.at[k % RING])
 
+    waiting = {}
+    names_recv = [arrival() for _ in ORDERS]
+
+    def send_names(source, first):
+        for j in range(3):
+            for order, step in ((1, 1), (2, 3), (3, 2)):
+                remote(
+                    source,
+                    lab.at[3 * j + order, pl.ds(first, 8)],
+                    neighbour(ORDERS[j][0], step),
+                    recv=names_recv[j],
+                )
+
     def make(k):
         gather_sums(k)
+        if k == 0:
+            for i in range(FT // 4):
+                get_feat[i].wait()
+                convert(4 * i)
+            pl.semaphore_wait(barrier, len(greeted))
+            waiting["give"] = remote(tile, lab.at[0, pl.ds(8, 8)], sibling)
+            waiting["keep"] = local(tile, lab.at[0, pl.ds(0, 8)])
+            send_names(tile, 0)
         result = product(a_high[...], a_low[...], f_high[...], f_low[...])
         for half in range(2):
             for u in range(STREAMS):
@@ -319,8 +341,8 @@
         stream.list_recv, stream.far_recv = arrival(), arrival()
 
     def make_table(j):
-        lab_down[j].wait_recv()
-        lab_far[j].wait_recv()
+        held_names = lab.at[pl.ds(1 + 3 * j, 3)]
+        pltpu.make_async_copy(held_names, held_names, names_recv[j]).wait()
         first, second, third = ORDERS[j]
         seen = jnp.concatenate([lab[0], lab[1 + 3 * j], lab[2 + 3 * j], lab[3 + 3 * j]], axis=0)
         row = lax.broadcasted_iota(I32, (64, LANES), 0)
@@ -588,34 +610,16 @@
         here = pl.ds(pl.multiple_of(first, ROWS), ROWS)
         last.append(remote(out_buf.at[u], out.at[pl.ds(1, SLOTS), here, :], sibling))
 
-    get_feat[0].wait()
-    convert(0)
-    get_feat[1].wait()
-    convert(8)
     get_col_tab.wait()
-    lab_up, lab_down, lab_far = {}, {}, {}
-    waiting = {}
 
     def product_block(k):
         make(k)
         if k == 0:
-            pl.semaphore_wait(barrier, len(greeted))
-            waiting["give"] = remote(tile, lab.at[0, pl.ds(8, 8)], sibling)
-            waiting["keep"] = local(tile, lab.at[0, pl.ds(0, 8)])
-        if k == 1:
-            waiting["keep"].wait()
             waiting["give"].wait_recv()
-            for j in range(3):
-                lab_up[j] = remote(lab.at[0], lab.at[1 + 3 * j], neighbour(ORDERS[j][0], 1))
-                lab_down[j] = remote(lab.at[0], lab.at[2 + 3 * j], neighbour(ORDERS[j][0], 3))
-        if k == 4:
-            for j in range(3):
-                lab_up[j].wait_recv()
-                lab_far[j] = remote(
-                    lab.at[1 + 3 * j], lab.at[3 + 3 * j], neighbour(ORDERS[j][0], 1)
-                )
+            send_names(lab.at[0, pl.ds(8, 8)], 8)
 
     def tables():
+        waiting["keep"].wait()
         for j in range(3):
             make_table(j)
         get_factor.wait()
@@ -630,11 +634,18 @@
         A3_MERGE: a3_merge, UPDATE: update, B3_FAR: b3_far, B2: b2_start, B2_FAR: b2_far,
         B1_FAR: b1_far, B1_NEAR: b1_near, B1_MERGE: b1_merge, FINISH: finish,
     }
+    paced = 0
     for kind, *numbers in ORDER:
+        if kind in PACED:
+            pl.semaphore_signal(pace_sem, inc=1, device_id=sibling, device_id_type=MESH)
+            if paced:
+                pl.semaphore_wait(pace_sem, 1)
+            paced += 1
         if kind in (MAKE, GIVE, TABLES):
             blocks_of[kind](*numbers)
         else:
             blocks_of[kind](streams[numbers[0]], *numbers[1:])
+    pl.semaphore_wait(pace_sem, 1)
     for copy in last:
         copy.wait_recv()
     for copy in sent:
@@ -689,6 +700,7 @@
         pltpu.SemaphoreType.DMA((N_SEND,)),
         pltpu.SemaphoreType.DMA((N_RECV,)),
         pltpu.SemaphoreType.DMA((N_LOCAL,)),
+        pltpu.SemaphoreType.REGULAR,
     ]
     hbm = pl.BlockSpec(memory_space=pl.ANY)
     held = pl.pallas_call(

time: 88.3 us -> 86.2 us (0.976)
  Pallas kernels: 87.6 us -> 85.5 us
    pallas_call x1, Pallas kernels: 86.3 us -> 84.3 us  [local_step(): pl.pallas_call(kernel, in_specs=[hbm] * 5, out_specs=pl.BlockSpec(memory_...]
where the time goes in v5:
time: 86.2 us; the launch traced here: 86.1 us
  Pallas kernels  85.5 us (99%)
    pallas_call x1, Pallas kernels, local_step(): pl.pallas_call(kernel, in_specs=[hbm] * 5, out_specs=pl.BlockSpec(memory_...  84.3 us

profile of v5, /device:TPU:1, one launch (start us, length us, event | category | flops | bytes accessed | tf_op | source)
XLA Modules:
  0.0 86.1 jit_solution(6339148526643576342)
XLA Ops:
  0.6 84.3 %shard_map.68.held = f32[7,128,512]{2,1,0:T(8,128)S(1)} custom-call(f32[6,128,4096]{2,1,0:T(8,128)} %blocks.1, f32[16,128,512]{2,1,0:T(8,128)} %features.1, s32[6,32]{1,0:T(8,128)} %col_ids.1, s32[6]{0:T(128)} %row_ids.1, f32[512,512]{1,0:T(8,128)} %factor.1), custom_call_target="tpu_custom_call" | custom-call | tf_op jit(solution)/shard_map/pallas_call | solution.py:706
  84.9 1.2 %shard_map.69 = (f32[128,512]{1,0:T(8,128)}, f32[6,128,512]{2,1,0:T(8,128)}) custom-call(f32[7,128,512]{2,1,0:T(8,128)S(1)} %shard_map.68.held), custom_call_target="tpu_custom_call" | custom-call | tf_op jit(solution)/shard_map/pallas_call | solution.py:716

commit v6 on v5

--- a/solution.py
+++ b/solution.py
@@ -25,6 +25,7 @@
 TILE_ROWS = ROWS * GROUPS
 SHIFT = {"z": 5, "y": 3, "x": 1}
 ORDERS = ("zyx", "yxz", "xzy")
+SECOND_ORDERS = ("zyx", "xzy", "yxz")
 PIECES = (
     ((0, 24), (24, 24), (48, 16)),
     ((0, 24), (24, 16), (40, 24)),
@@ -66,8 +67,8 @@
     ("b1_got", 24),
 )
 STREAM_SLOTS = 36 + 24 + 6 + 6 + 24 + 36
-N_SEND = 36
-N_RECV = 110
+N_SEND = 35
+N_RECV = 96
 N_LOCAL = 16
 RING = 4
 VMEM_LIMIT = 58 << 20
@@ -143,6 +144,16 @@
         to[axis] = (at[axis] + step) % 4
         return (to["z"], to["y"] * 8 + to["x"] * 2 + core)
 
+    def blend(first, second):
+        return first if first is second else first + core * (second - first)
+
+    def ring(number, phase, step):
+        here = neighbour(ORDERS[number][phase], step)
+        there = neighbour(SECOND_ORDERS[number][phase], step)
+        if ORDERS[number] == SECOND_ORDERS[number]:
+            return here
+        return tuple(blend(a, b) for a, b in zip(here, there))
+
     sibling = (z, gy - core + (1 - core))
     counts = {"send": 0, "recv": 0, "local": 0}
     sent = []
@@ -160,7 +171,7 @@
         stream.send = send_sem.at[take("send", N_SEND)]
         for p in stream.pieces:
             p.stream = stream
-            p.ways = [(neighbour(axis, 1), neighbour(axis, 3)) for axis in ORDERS[p.number]]
+            p.ways = [(ring(p.number, i, 1), ring(p.number, i, 3)) for i in range(3)]
 
     def remote(source, target, device, stream=None, recv=None):
         copy = pltpu.make_async_remote_copy(
@@ -260,7 +271,7 @@
                 remote(
                     source,
                     lab.at[3 * j + order, pl.ds(first, 8)],
-                    neighbour(ORDERS[j][0], step),
+                    ring(j, 0, step),
                     recv=names_recv[j],
                 )
 
@@ -343,7 +354,10 @@
     def make_table(j):
         held_names = lab.at[pl.ds(1 + 3 * j, 3)]
         pltpu.make_async_copy(held_names, held_names, names_recv[j]).wait()
-        first, second, third = ORDERS[j]
+        own = [blend(at[a], at[b]) for a, b in zip(ORDERS[j], SECOND_ORDERS[j])]
+        stride = [
+            blend(1 << SHIFT[a], 1 << SHIFT[b]) for a, b in zip(ORDERS[j], SECOND_ORDERS[j])
+        ]
         seen = jnp.concatenate([lab[0], lab[1 + 3 * j], lab[2 + 3 * j], lab[3 + 3 * j]], axis=0)
         row = lax.broadcasted_iota(I32, (64, LANES), 0)
         lane = lax.broadcasted_iota(I32, (64, LANES), 1)
@@ -362,19 +376,25 @@
             return jnp.where(step == 0, 0, jnp.where(step == 3, 1, step + 1))
 
         named = (
-            (at[first] << SHIFT[first])
-            + (((at[second] + step_of((lane >> 3) & 3)) & 3) << SHIFT[second])
-            + (((at[third] + step_of((lane >> 1) & 3)) & 3) << SHIFT[third])
+            own[0] * stride[0]
+            + ((own[1] + step_of((lane >> 3) & 3)) & 3) * stride[1]
+            + ((own[2] + step_of((lane >> 1) & 3)) & 3) * stride[2]
             + (lane & 1)
         )
         last = jnp.max(jnp.where(seen == named, place_of_row, 0), axis=0, keepdims=True)
+        at_axis = [
+            (wanted >> SHIFT[a]) & 3
+            if ORDERS[j] == SECOND_ORDERS[j]
+            else blend((wanted >> SHIFT[a]) & 3, (wanted >> SHIFT[b]) & 3)
+            for a, b in zip(ORDERS[j], SECOND_ORDERS[j])
+        ]
         place = (
             1
-            + order_of((((wanted >> SHIFT[second]) & 3) - at[second]) & 3) * 8
-            + order_of((((wanted >> SHIFT[third]) & 3) - at[third]) & 3) * 2
+            + order_of((at_axis[1] - own[1]) & 3) * 8
+            + order_of((at_axis[2] - own[2]) & 3) * 2
             + (wanted & 1)
         )
-        place = jnp.where(((wanted >> SHIFT[first]) & 3) == at[first], place, 0)
+        place = jnp.where(at_axis[0] == own[0], place, 0)
         tab_v[j] = jnp.where(line == 0, previous, jnp.where(line == 1, last, place))
 
     def add_list(stream, order):

time: 86.2 us -> 85.8 us (level)
  no operation moved by 1% of the time
where the time goes in v6:
time: 85.8 us; the launch traced here: 85.7 us
  Pallas kernels  85.1 us (99%)
    pallas_call x1, Pallas kernels, local_step(): pl.pallas_call(kernel, in_specs=[hbm] * 5, out_specs=pl.BlockSpec(memory_...  83.8 us

profile of v6, /device:TPU:1, one launch (start us, length us, event | category | flops | bytes accessed | tf_op | source)
XLA Modules:
  0.0 85.7 jit_solution(8371052941418313266)
XLA Ops:
  0.6 83.8 %shard_map.68.held = f32[7,128,512]{2,1,0:T(8,128)S(1)} custom-call(f32[6,128,4096]{2,1,0:T(8,128)} %blocks.1, f32[16,128,512]{2,1,0:T(8,128)} %features.1, s32[6,32]{1,0:T(8,128)} %col_ids.1, s32[6]{0:T(128)} %row_ids.1, f32[512,512]{1,0:T(8,128)} %factor.1), custom_call_target="tpu_custom_call" | custom-call | tf_op jit(solution)/shard_map/pallas_call | solution.py:726
  84.5 1.2 %shard_map.69 = (f32[128,512]{1,0:T(8,128)}, f32[6,128,512]{2,1,0:T(8,128)}) custom-call(f32[7,128,512]{2,1,0:T(8,128)S(1)} %shard_map.68.held), custom_call_target="tpu_custom_call" | custom-call | tf_op jit(solution)/shard_map/pallas_call | solution.py:736
